TPU v7x, 128 devices: a whole 4x4x4 slice. The times are simulated.
128 devices in a mesh: gx: 8 (over x, core), gy: 4 (over z), gz: 4 (over y).
Axes of the slice: x: 4, y: 4, z: 4, core: 2. Of those that a mesh axis runs over, the one named last changes fastest.
Arguments:
- right_side: float32 [512, 256, 1024], P('gx', 'gy', 'gz'), may hold values from -5 to 7
- initial_guess: float32 [512, 256, 1024], P('gx', 'gy', 'gz'), may hold values from -5 to 7
Outputs:
- solution: float32 [512, 256, 1024], P('gx', 'gy', 'gz')
All inputs are finite; a program needn't handle non-finite values.
Results may differ from a plain program's by a relative error of at most 0.000028.
Values sent between devices are 32-bit elements; how exact they have to be, the bound alone decides.
A program may use at most 128 MiB of HBM per device.

v0:
```python
import jax
import jax.numpy as jnp
from jax import lax
from jax.sharding import Mesh
from jax.sharding import PartitionSpec as P

COARSE_SWEEPS = 6
GX = ("gx_0", "gx_1")
GX_GY_GZ = ("gx_0", "gx_1", "gy", "gz")


relax_weight = 0.8


def passed_along(shard, axis, by):
    devices = lax.axis_size(axis)
    return lax.ppermute(shard, axis, [(i, (i + by) % devices) for i in range(devices)])


def extended_2(shard, sides, width):
    edges = {}
    for axis, dim in sides:
        devices, length = (lax.axis_size(axis), shard.shape[dim])
        up = [(i, (i + 1) % devices) for i in range(devices)]
        last = lax.slice_in_dim(shard, length - width, length, axis=dim)
        first = lax.slice_in_dim(shard, 0, width, axis=dim)
        edges[dim] = (
            lax.ppermute(last, axis, up),
            lax.ppermute(first, axis, [(b, a) for a, b in up]),
        )
    done = []
    for _, dim in sides:
        low, high = edges[dim]
        around = [(width, width) if d in done else (0, 0) for d in range(shard.ndim)]
        shard = jnp.concatenate([jnp.pad(low, around), shard, jnp.pad(high, around)], axis=dim)
        done.append(dim)
    return shard


def joined_along(parts, dim):
    dims = list(parts.shape[1:])
    dims[dim] *= parts.shape[0]
    return jnp.moveaxis(parts, 0, dim).reshape(dims)


def sent_to_all(shard, axis):
    copies = jnp.broadcast_to(shard, (lax.axis_size(axis), *shard.shape))
    return lax.all_to_all(copies, axis, split_axis=0, concat_axis=0, tiled=True)


def collect(shard, axis, dim):
    return joined_along(sent_to_all(shard, axis), dim)


def padded_2(block, sides, width):
    for axis, dim in sides:
        count = lax.axis_size(axis)
        forward = [(i, i + 1) for i in range(count - 1)]
        forward.append((count - 1, 0))
        backward = [(target, source) for source, target in forward]
        low = lax.ppermute(
            lax.slice_in_dim(block, block.shape[dim] - width, None, axis=dim), axis, forward
        )
        high = lax.ppermute(lax.slice_in_dim(block, 0, width, axis=dim), axis, backward)
        block = jnp.concatenate([low, block, high], axis=dim)
    return block


def one_axis_at_a_time(shard, axes):
    for axis in axes:
        shard = lax.psum(shard, axis)
    return shard


def stencil_parts(padded):
    centre = padded[1:-1, 1:-1, 1:-1]
    beside = padded[2:, 1:-1, 1:-1] + padded[:-2, 1:-1, 1:-1]
    beside = beside + padded[1:-1, 2:, 1:-1] + padded[1:-1, :-2, 1:-1]
    beside = beside + padded[1:-1, 1:-1, 2:] + padded[1:-1, 1:-1, :-2]
    return (centre, beside)


def relax_step(centre, beside, source, level_scale):
    return centre + relax_weight * (source / (6.0 * level_scale) - centre + beside / 6.0)


def defect_of(centre, beside, source, level_scale):
    return source - level_scale * (6.0 * centre - beside)


def restrict_along(extended, along):
    inner_count = extended.shape[along] - 1
    lower_side = lax.slice_in_dim(extended, 0, inner_count, 2, along)
    on_points = lax.slice_in_dim(extended, 1, inner_count + 1, 2, along)
    upper_side = lax.slice_in_dim(extended, 2, inner_count + 1, 2, along)
    return 0.25 * lower_side + 0.5 * on_points + 0.25 * upper_side


def restrict_lower(values):
    rim = passed_along(values[-1:], GX, 1)
    values = restrict_along(jnp.concatenate([rim, values], 0), 0)
    rim = passed_along(values[:, -1:], "gy", 1)
    values = restrict_along(jnp.concatenate([rim, values], 1), 1)
    rim = passed_along(values[:, :, -1:], "gz", 1)
    return restrict_along(jnp.concatenate([rim, values], 2), 2)


def prolong_along(values, rim, along):
    upper_side = jnp.concatenate(
        [lax.slice_in_dim(values, 1, values.shape[along], 1, along), rim], along
    )
    between = 0.5 * (values + upper_side)
    stacked = jnp.stack([values, between], along + 1)
    new_shape = list(values.shape)
    new_shape[along] = 2 * new_shape[along]
    return stacked.reshape(new_shape)


def prolong_upper(values):
    rim = passed_along(values[:1], GX, -1)
    values = prolong_along(values, rim, 0)
    rim = passed_along(values[:, :1], "gy", -1)
    values = prolong_along(values, rim, 1)
    rim = passed_along(values[:, :, :1], "gz", -1)
    return prolong_along(values, rim, 2)


def near_faces(values):
    return extended_2(values, ((GX, 0), ("gy", 1), ("gz", 2)), 1)


def single_sweep(approx, source, level_scale):
    centre, beside = stencil_parts(near_faces(approx))
    return relax_step(centre, beside, source, level_scale)


def paired_sweeps(approx, source, level_scale):
    approx = single_sweep(approx, source, level_scale)
    return single_sweep(approx, source, level_scale)


def coarse_relax(padded, approx, source):
    beside = padded[2:, 1:-1] + padded[:-2, 1:-1]
    beside = beside + padded[1:-1, 2:] + padded[1:-1, :-2]
    beside = beside + jnp.roll(approx, -1, 2) + jnp.roll(approx, 1, 2)
    return relax_step(approx, beside, source, 0.0625)


def coarsest_solve(source):
    thickness = source.shape[2]
    whole_source = collect(source, "gz", 2)
    margin = COARSE_SWEEPS - 1
    padded_source = padded_2(whole_source, ((GX, 0), ("gy", 1)), margin)
    empty = jnp.zeros_like(padded_source)
    approx = relax_step(empty, empty, padded_source, 0.0625)
    size_first = padded_source.shape[0]
    size_second = padded_source.shape[1]
    for sweep_index in range(margin):
        inner = sweep_index + 1
        inner_source = padded_source[inner : size_first - inner, inner : size_second - inner]
        approx = coarse_relax(approx, approx[1:-1, 1:-1], inner_source)
    return lax.dynamic_slice_in_dim(approx, lax.axis_index("gz") * thickness, thickness, 2)


def multigrid_cycle(approx, source, grid_level):
    if grid_level == 2:
        return coarsest_solve(source)
    level_scale = 0.25**grid_level
    approx = paired_sweeps(approx, source, level_scale)
    centre, beside = stencil_parts(near_faces(approx))
    defect_field = defect_of(centre, beside, source, level_scale)
    coarse_source = restrict_lower(defect_field)
    correction = multigrid_cycle(jnp.zeros_like(coarse_source), coarse_source, grid_level + 1)
    approx = approx + prolong_upper(correction)
    return paired_sweeps(approx, source, level_scale)


def shards(right_side, initial_guess):
    cell_count = right_side.size * lax.axis_size(GX) * lax.axis_size("gy") * lax.axis_size("gz")
    totals = (
        one_axis_at_a_time(jnp.sum(right_side), GX_GY_GZ),
        one_axis_at_a_time(jnp.sum(initial_guess), GX_GY_GZ),
    )
    source = right_side - totals[0] / cell_count
    approx = initial_guess - totals[1] / cell_count
    return multigrid_cycle(approx, source, 0)


def solution(mesh):
    torus = Mesh(
        mesh.devices.reshape(4, 2, mesh.shape["gy"], mesh.shape["gz"]), ("gx_0", "gx_1", "gy", "gz")
    )
    placed = (P(GX, "gy", "gz"), P(GX, "gy", "gz"))
    return jax.shard_map(
        shards, mesh=torus, in_specs=placed, out_specs=P(GX, "gy", "gz"), check_vma=False
    )
```

profile of v0, /device:TPU:0, one launch (start us, length us, event | category | flops | bytes accessed | tf_op | source)
XLA Modules:
  0.0 562.2 jit_solution(9182305907823817487)
XLA Ops:
  0.0 3.9 reduce_sum.19
  3.9 3.9 reduce_sum.18
  7.8 11.2 %all-reduce.44 = (f32[]{:T(128)}, f32[]{:T(128)}) all-reduce(f32[]{:T(128)} %reduce_sum.18, f32[]{:T(128)} %reduce_sum.19), channel_id=1, replica_groups=mesh['gx_0'=4,'gx_1'=2,'gy'=4,'gz'=4] {'gx_0'}, use_global_device_ids=true, to_apply=%region_1.0 | all-reduce | flops 2 | bytes 16 | tf_op jit(solution)/shard_map/psum | solution.py:71
  19.0 3.1 all-reduce.45
  22.1 12.4 %all-reduce.43 = (f32[]{:T(128)}, f32[]{:T(128)}) all-reduce(f32[]{:T(128)} %get-tuple-element.11, f32[]{:T(128)} %get-tuple-element.12), channel_id=1, replica_groups=mesh['gx_0'=4,'gx_1'=2,'gy'=4,'gz'=4] {'gy'}, use_global_device_ids=true, to_apply=%region_3.0 | all-reduce | flops 2 | bytes 16 | tf_op jit(solution)/shard_map/psum | solution.py:71
  34.5 11.4 %all-reduce.42 = (f32[]{:T(128)}, f32[]{:T(128)}) all-reduce(f32[]{:T(128)} %get-tuple-element.7, f32[]{:T(128)} %get-tuple-element.8), channel_id=1, replica_groups=mesh['gx_0'=4,'gx_1'=2,'gy'=4,'gz'=4] {'gz'}, use_global_device_ids=true, to_apply=%region_4.0 | all-reduce | flops 2 | bytes 16 | tf_op jit(solution)/shard_map/psum | solution.py:71
  49.1 2.9 collective-permute-start
  52.2 3.2 collective-permute-start.2
  60.6 3.2 collective-permute-done.4
  65.0 3.9 collective-permute-done.5
  71.1 22.0 %fusion.47 = f32[64,64,256]{2,1,0:T(8,128)S(1)} fusion(f32[64,64,256]{2,1,0:T(8,128)} %copy-done.1, f32[64,64,1]{2,1,0:T(8,128)} %copy.28, f32[66,1,256]{2,1,0:T(1,128)S(1)} %pad.126, f32[66,1,256]{2,1,0:T(1,128)S(1)} %pad.127, f32[1,64,256]{2,1,0:T(8,128)S(1)} %collective-permute-done, f32[1,64,256]{2,1,0:T(8,128)S(1)} %collective-permute-done.1, ...), kind=kLoop, calls=%fused_computation.121 | loop fusion | flops 37748736 | bytes 12881924 | tf_op jit(solution)/shard_map/add | solution.py:84
  93.2 2.9 collective-permute-start.6
  96.2 3.2 collective-permute-start.8
  104.5 3.2 collective-permute-done.10
  108.6 4.4 collective-permute-done.11
  115.2 22.0 %fusion.36 = f32[64,64,256]{2,1,0:T(8,128)S(1)} fusion(f32[64,64,256]{2,1,0:T(8,128)} %copy-done.4, f32[64,64,1]{2,1,0:T(8,128)} %copy.32, f32[66,1,256]{2,1,0:T(1,128)S(1)} %pad.130, f32[66,1,256]{2,1,0:T(1,128)S(1)} %pad.131, f32[1,64,256]{2,1,0:T(8,128)S(1)} %collective-permute-done.6, f32[1,64,256]{2,1,0:T(8,128)S(1)} %collective-permute-done.7, ...), kind=kLoop, calls=%fused_computation.92 | loop fusion | flops 37748736 | bytes 12881924 | tf_op jit(solution)/shard_map/add | solution.py:84
  137.4 3.2 collective-permute-start.14
  140.6 3.0 collective-permute-start.12
  148.7 3.2 collective-permute-done.16
  152.6 4.4 collective-permute-done.17
  159.2 21.7 %fusion.25 = f32[64,64,256]{2,1,0:T(8,128)S(1)} fusion(f32[64,64,1]{2,1,0:T(8,128)} %copy.36, f32[66,1,256]{2,1,0:T(1,128)S(1)} %pad.134, f32[66,1,256]{2,1,0:T(1,128)S(1)} %pad.135, f32[1,64,256]{2,1,0:T(8,128)S(1)} %collective-permute-done.12, f32[64,64,256]{2,1,0:T(8,128)} %copy-done, f32[1,64,256]{2,1,0:T(8,128)S(1)} %collective-permute-done.13, ...), kind=kLoop, calls=%fused_computation.63 | loop fusion | flops 34603008 | bytes 12881924 | tf_op jit(solution)/shard_map/sub | solution.py:88
  181.0 4.9 collective-permute-done.18
  187.5 3.3 collective-permute-start.23
  195.8 4.1 slice.756
  201.7 2.9 collective-permute-start.21
  205.6 3.3 collective-permute-start.25
  208.9 19.6 %slice.762 = f32[32,32,128]{2,1,0:T(8,128)S(1)} slice(f32[32,32,256]{2,1,0:T(8,128)S(1)} %multiply_add_fusion.1), slice={[0:32:1], [0:32:1], [1:256:2]} | slice | bytes 1048576 | tf_op jit(solution)/shard_map/slice | solution.py:95
  228.5 20.0 %slice.761 = f32[32,32,128]{2,1,0:T(8,128)} slice(f32[32,32,256]{2,1,0:T(8,128)S(1)} %multiply_add_fusion.1), slice={[0:32:1], [0:32:1], [0:256:2]} | slice | bytes 1048576 | tf_op jit(solution)/shard_map/slice | solution.py:94
  250.0 19.5 %slice.760 = f32[32,32,128]{2,1,0:T(8,128)S(1)} slice(f32[32,32,257]{2,1,0:T(8,128)S(1)} %pad_maximum_fusion.84), slice={[0:32:1], [0:32:1], [0:256:2]} | slice | bytes 1048576 | tf_op jit(solution)/shard_map/slice | solution.py:93
  271.6 2.9 collective-permute-start.27
  274.6 3.7 collective-permute-start.29
  280.6 8.8 %collective-permute-done.31 = f32[32,32,1]{2,1,0:T(8,128)S(1)} collective-permute-done((f32[32,32,1]{2,1,0:T(8,128)S(1)}, f32[32,32,1]{2,1,0:T(8,128)S(1)}, u32[]{:S(2)}, u32[]{:S(2)}) %collective-permute-start.31) | collective-permute-done | bytes 4128 | tf_op jit(solution)/shard_map/ppermute | solution.py:29
  289.4 2.9 collective-permute-done.32
  293.1 3.2 collective-permute-start.35
  296.3 3.0 collective-permute-start.33
  301.6 9.3 %collective-permute-done.37 = f32[32,32,1]{2,1,0:T(8,128)S(1)} collective-permute-done((f32[32,32,1]{2,1,0:T(8,128)S(1)}, f32[32,32,1]{2,1,0:T(8,128)S(1)}, u32[]{:S(2)}, u32[]{:S(2)}) %collective-permute-start.37) | collective-permute-done | bytes 4128 | tf_op jit(solution)/shard_map/ppermute | solution.py:29
  312.9 4.4 collective-permute-done.39
  317.7 4.7 collective-permute-done.40
  331.7 9.5 %all_to_all.5 = f32[4,1,16384]{2,1,0:T(1,128)S(1)} all-to-all(f32[4,1,16384]{2,1,0:T(1,128)S(1)} %reshape.186), channel_id=1, replica_groups=mesh['gx_0'=4,'gx_1'=2,'gy'=4,'gz'=4] {'gz'}, dimensions={0} | all-to-all | bytes 524288 | tf_op jit(solution)/shard_map/all_to_all | solution.py:48
  344.5 2.9 collective-permute-start.43
  349.6 3.4 collective-permute-start.45
  353.0 3.7 collective-permute-done.44
  364.0 3.2 collective-permute-start.47
  370.4 10.0 %collective-permute-done.48 = f32[32,32,1]{2,0,1:T(8,128)S(1)} collective-permute-done((f32[32,32,1]{2,0,1:T(8,128)S(1)}, f32[32,32,1]{2,0,1:T(8,128)S(1)}, u32[]{:S(2)}, u32[]{:S(2)}) %collective-permute-start.48) | collective-permute-done | bytes 4128 | tf_op jit(solution)/shard_map/ppermute | solution.py:17
  382.5 3.0 copy.45
  388.8 2.9 collective-permute-start.49
  391.8 3.2 collective-permute-start.51
  397.7 8.7 %collective-permute-done.53 = f32[32,32,1]{2,1,0:T(8,128)S(1)} collective-permute-done((f32[32,32,1]{2,1,0:T(8,128)S(1)}, f32[32,32,1]{2,1,0:T(8,128)S(1)}, u32[]{:S(2)}, u32[]{:S(2)}) %collective-permute-start.53) | collective-permute-done | bytes 4128 | tf_op jit(solution)/shard_map/ppermute | solution.py:29
  406.4 3.3 collective-permute-done.54
  410.4 2.9 collective-permute-start.55
  413.3 3.4 collective-permute-start.57
  419.1 8.8 %collective-permute-done.59 = f32[32,32,1]{2,1,0:T(8,128)S(1)} collective-permute-done((f32[32,32,1]{2,1,0:T(8,128)S(1)}, f32[32,32,1]{2,1,0:T(8,128)S(1)}, u32[]{:S(2)}, u32[]{:S(2)}) %collective-permute-start.59) | collective-permute-done | bytes 4128 | tf_op jit(solution)/shard_map/ppermute | solution.py:29
  433.0 3.4 collective-permute-done.62
  451.2 9.2 %copy.54 = f32[64,64,128,2]{1,0,3,2:T(8,128)} copy(f32[64,64,128,2]{2,0,1,3:T(8,128)} %pad_maximum_fusion.81) | data formatting | bytes 8388608 | tf_op jit(solution)/shard_map/stack | solution.py:113
  460.5 7.7 %copy.55 = f32[64,64,256]{2,1,0:T(8,128)} copy(f32[64,64,256]{1,0,2:T(8,128)} %bitcast.42) | data formatting | bytes 8388608 | tf_op jit(solution)/shard_map/reshape | solution.py:116
  468.2 4.3 add.597
  472.7 2.9 collective-permute-start.64
  476.0 3.2 collective-permute-start.66
  488.3 4.4 collective-permute-done.69
  494.8 22.0 %fusion.16 = f32[64,64,256]{2,1,0:T(8,128)S(1)} fusion(f32[64,64,256]{2,1,0:T(8,128)} %copy-done.2, f32[64,64,1]{2,1,0:T(8,128)} %copy.59, f32[66,1,256]{2,1,0:T(1,128)S(1)} %pad.158, f32[66,1,256]{2,1,0:T(1,128)S(1)} %pad.159, f32[1,64,256]{2,1,0:T(8,128)S(1)} %collective-permute-done.64, f32[1,64,256]{2,1,0:T(8,128)S(1)} %collective-permute-done.65, ...), kind=kLoop, calls=%fused_computation.36 | loop fusion | flops 37748736 | bytes 12881924 | tf_op jit(solution)/shard_map/add | solution.py:84
  517.0 2.9 collective-permute-start.70
  520.0 3.2 collective-permute-start.72
  532.4 4.4 collective-permute-done.75
  539.0 23.0 %fusion.5 = f32[64,64,256]{2,1,0:T(8,128)} fusion(f32[64,64,256]{2,1,0:T(8,128)} %copy-done.3, f32[64,64,1]{2,1,0:T(8,128)} %copy.63, f32[66,1,256]{2,1,0:T(1,128)S(1)} %pad.162, f32[66,1,256]{2,1,0:T(1,128)S(1)} %pad.163, f32[1,64,256]{2,1,0:T(8,128)S(1)} %collective-permute-done.70, f32[1,64,256]{2,1,0:T(8,128)S(1)} %collective-permute-done.71, ...), kind=kLoop, calls=%fused_computation.7 | loop fusion | flops 37748736 | bytes 12881924 | tf_op jit(solution)/shard_map/add | solution.py:84
  (284 shorter events, 126.8 us)
Async XLA Ops:
  49.1 22.0 %collective-permute-start.1 = (f32[1,64,256]{2,1,0:T(8,128)S(1)}, f32[1,64,256]{2,1,0:T(8,128)S(1)}, u32[]{:S(2)}, u32[]{:S(2)}) collective-permute-start(f32[1,64,256]{2,1,0:T(8,128)S(1)} %get-tuple-element.41), channel_id=1, source_target_pairs={{0,16},{16,32},{32,48},{48,64},{64,80},{80,96},{96,112},{112,0},{1... | collective-permute-start | bytes 196616 | tf_op jit(solution)/shard_map/ppermute | solution.py:28
  49.1 22.0 %collective-permute-start = (f32[1,64,256]{2,1,0:T(8,128)S(1)}, f32[1,64,256]{2,1,0:T(8,128)S(1)}, u32[]{:S(2)}, u32[]{:S(2)}) collective-permute-start(f32[1,64,256]{2,1,0:T(8,128)S(1)} %get-tuple-element.42), channel_id=1, source_target_pairs={{16,0},{32,16},{48,32},{64,48},{80,64},{96,80},{112,96},{0,112},{1... | collective-permute-start | bytes 196616 | tf_op jit(solution)/shard_map/ppermute | solution.py:29
  52.1 18.8 %collective-permute-start.3 = (f32[64,1,256]{2,1,0:T(1,128)S(1)}, f32[64,1,256]{2,1,0:T(1,128)S(1)}, u32[]{:S(2)}, u32[]{:S(2)}) collective-permute-start(f32[64,1,256]{2,1,0:T(1,128)S(1)} %get-tuple-element.43), channel_id=1, source_target_pairs={{0,4},{4,8},{8,12},{12,0},{1,5},{5,9},{9,13},{13,1},{2,6},{6,10},{... | collective-permute-start | bytes 196616 | tf_op jit(solution)/shard_map/ppermute | solution.py:28
  52.2 18.8 %collective-permute-start.2 = (f32[64,1,256]{2,1,0:T(1,128)S(1)}, f32[64,1,256]{2,1,0:T(1,128)S(1)}, u32[]{:S(2)}, u32[]{:S(2)}) collective-permute-start(f32[64,1,256]{2,1,0:T(1,128)S(1)} %get-tuple-element.44), channel_id=1, source_target_pairs={{4,0},{8,4},{12,8},{0,12},{5,1},{9,5},{13,9},{1,13},{6,2},{10,6},{... | collective-permute-start | bytes 196616 | tf_op jit(solution)/shard_map/ppermute | solution.py:29
  63.8 5.1 collective-permute-start.5
  93.2 22.0 %collective-permute-start.7 = (f32[1,64,256]{2,1,0:T(8,128)S(1)}, f32[1,64,256]{2,1,0:T(8,128)S(1)}, u32[]{:S(2)}, u32[]{:S(2)}) collective-permute-start(f32[1,64,256]{2,1,0:T(8,128)S(1)} %get-tuple-element.35), channel_id=1, source_target_pairs={{0,16},{16,32},{32,48},{48,64},{64,80},{80,96},{96,112},{112,0},{1... | collective-permute-start | bytes 196616 | tf_op jit(solution)/shard_map/ppermute | solution.py:28
  93.2 22.0 %collective-permute-start.6 = (f32[1,64,256]{2,1,0:T(8,128)S(1)}, f32[1,64,256]{2,1,0:T(8,128)S(1)}, u32[]{:S(2)}, u32[]{:S(2)}) collective-permute-start(f32[1,64,256]{2,1,0:T(8,128)S(1)} %get-tuple-element.36), channel_id=1, source_target_pairs={{16,0},{32,16},{48,32},{64,48},{80,64},{96,80},{112,96},{0,112},{1... | collective-permute-start | bytes 196616 | tf_op jit(solution)/shard_map/ppermute | solution.py:29
  96.2 18.9 %collective-permute-start.9 = (f32[64,1,256]{2,1,0:T(1,128)S(1)}, f32[64,1,256]{2,1,0:T(1,128)S(1)}, u32[]{:S(2)}, u32[]{:S(2)}) collective-permute-start(f32[64,1,256]{2,1,0:T(1,128)S(1)} %get-tuple-element.37), channel_id=1, source_target_pairs={{0,4},{4,8},{8,12},{12,0},{1,5},{5,9},{9,13},{13,1},{2,6},{6,10},{... | collective-permute-start | bytes 196616 | tf_op jit(solution)/shard_map/ppermute | solution.py:28
  96.2 18.9 %collective-permute-start.8 = (f32[64,1,256]{2,1,0:T(1,128)S(1)}, f32[64,1,256]{2,1,0:T(1,128)S(1)}, u32[]{:S(2)}, u32[]{:S(2)}) collective-permute-start(f32[64,1,256]{2,1,0:T(1,128)S(1)} %get-tuple-element.38), channel_id=1, source_target_pairs={{4,0},{8,4},{12,8},{0,12},{5,1},{9,5},{13,9},{1,13},{6,2},{10,6},{... | collective-permute-start | bytes 196616 | tf_op jit(solution)/shard_map/ppermute | solution.py:29
  107.7 5.3 collective-permute-start.11
  137.3 21.8 %collective-permute-start.15 = (f32[64,1,256]{2,1,0:T(1,128)S(1)}, f32[64,1,256]{2,1,0:T(1,128)S(1)}, u32[]{:S(2)}, u32[]{:S(2)}) collective-permute-start(f32[64,1,256]{2,1,0:T(1,128)S(1)} %get-tuple-element.31), channel_id=1, source_target_pairs={{0,4},{4,8},{8,12},{12,0},{1,5},{5,9},{9,13},{13,1},{2,6},{6,10},{... | collective-permute-start | bytes 196616 | tf_op jit(solution)/shard_map/ppermute | solution.py:28
  137.4 21.7 %collective-permute-start.14 = (f32[64,1,256]{2,1,0:T(1,128)S(1)}, f32[64,1,256]{2,1,0:T(1,128)S(1)}, u32[]{:S(2)}, u32[]{:S(2)}) collective-permute-start(f32[64,1,256]{2,1,0:T(1,128)S(1)} %get-tuple-element.32), channel_id=1, source_target_pairs={{4,0},{8,4},{12,8},{0,12},{5,1},{9,5},{13,9},{1,13},{6,2},{10,6},{... | collective-permute-start | bytes 196616 | tf_op jit(solution)/shard_map/ppermute | solution.py:29
  140.6 18.6 %collective-permute-start.13 = (f32[1,64,256]{2,1,0:T(8,128)S(1)}, f32[1,64,256]{2,1,0:T(8,128)S(1)}, u32[]{:S(2)}, u32[]{:S(2)}) collective-permute-start(f32[1,64,256]{2,1,0:T(8,128)S(1)} %get-tuple-element.29), channel_id=1, source_target_pairs={{0,16},{16,32},{32,48},{48,64},{64,80},{80,96},{96,112},{112,0},{1... | collective-permute-start | bytes 196616 | tf_op jit(solution)/shard_map/ppermute | solution.py:28
  140.6 18.6 %collective-permute-start.12 = (f32[1,64,256]{2,1,0:T(8,128)S(1)}, f32[1,64,256]{2,1,0:T(8,128)S(1)}, u32[]{:S(2)}, u32[]{:S(2)}) collective-permute-start(f32[1,64,256]{2,1,0:T(8,128)S(1)} %get-tuple-element.30), channel_id=1, source_target_pairs={{16,0},{32,16},{48,32},{64,48},{80,64},{96,80},{112,96},{0,112},{1... | collective-permute-start | bytes 196616 | tf_op jit(solution)/shard_map/ppermute | solution.py:29
  151.9 5.1 collective-permute-start.17
  187.1 7.0 %collective-permute-start.19 = (f32[32,1,256]{2,1,0:T(1,128)S(1)}, f32[32,1,256]{2,1,0:T(1,128)S(1)}, u32[]{:S(2)}, u32[]{:S(2)}) collective-permute-start(f32[32,1,256]{2,1,0:T(1,128)S(1)} %slice.939), channel_id=1, source_target_pairs={{0,4},{4,8},{8,12},{12,0},{1,5},{5,9},{9,13},{13,1},{2,6},{6,10},{... | collective-permute-start | bytes 98312 | tf_op jit(solution)/shard_map/ppermute | solution.py:17
  187.2 17.4 %collective-permute-start.24 = (f32[32,1,128]{2,1,0:T(1,128)S(1)}, f32[32,1,128]{2,1,0:T(1,128)S(1)}, u32[]{:S(2)}, u32[]{:S(2)}) collective-permute-start(f32[32,1,128]{2,1,0:T(1,128)S(1)} %broadcast.195), channel_id=1, source_target_pairs={{0,4},{4,8},{8,12},{12,0},{1,5},{5,9},{9,13},{13,1},{2,6},{6,10},{... | collective-permute-start | bytes 49160 | tf_op jit(solution)/shard_map/ppermute | solution.py:28
  187.5 18.0 %collective-permute-start.23 = (f32[32,1,128]{2,1,0:T(1,128)S(1)}, f32[32,1,128]{2,1,0:T(1,128)S(1)}, u32[]{:S(2)}, u32[]{:S(2)}) collective-permute-start(f32[32,1,128]{2,1,0:T(1,128)S(1)} %broadcast.195), channel_id=1, source_target_pairs={{4,0},{8,4},{12,8},{0,12},{5,1},{9,5},{13,9},{1,13},{6,2},{10,6},{... | collective-permute-start | bytes 49160 | tf_op jit(solution)/shard_map/ppermute | solution.py:29
  201.6 46.8 %collective-permute-start.20 = (f32[32,32,1]{2,1,0:T(8,128)S(1)}, f32[32,32,1]{2,1,0:T(8,128)}, u32[]{:S(2)}, u32[]{:S(2)}) collective-permute-start(f32[32,32,1]{2,1,0:T(8,128)S(1)} %slice.940), channel_id=1, source_target_pairs={{0,1},{1,2},{2,3},{3,0},{4,5},{5,6},{6,7},{7,4},{8,9},{9,10},{10,1... | collective-permute-start | bytes 12296 | tf_op jit(solution)/shard_map/ppermute | solution.py:17
  201.7 67.8 %collective-permute-start.22 = (f32[1,32,128]{2,1,0:T(8,128)S(1)}, f32[1,32,128]{2,1,0:T(8,128)S(1)}, u32[]{:S(2)}, u32[]{:S(2)}) collective-permute-start(f32[1,32,128]{2,1,0:T(8,128)S(1)} %broadcast.194), channel_id=1, source_target_pairs={{0,16},{16,32},{32,48},{48,64},{64,80},{80,96},{96,112},{112,0},{1... | collective-permute-start | bytes 49160 | tf_op jit(solution)/shard_map/ppermute | solution.py:28
  201.7 67.8 %collective-permute-start.21 = (f32[1,32,128]{2,1,0:T(8,128)S(1)}, f32[1,32,128]{2,1,0:T(8,128)S(1)}, u32[]{:S(2)}, u32[]{:S(2)}) collective-permute-start(f32[1,32,128]{2,1,0:T(8,128)S(1)} %broadcast.194), channel_id=1, source_target_pairs={{16,0},{32,16},{48,32},{64,48},{80,64},{96,80},{112,96},{0,112},{1... | collective-permute-start | bytes 49160 | tf_op jit(solution)/shard_map/ppermute | solution.py:29
  205.5 64.0 %collective-permute-start.26 = (f32[32,32,1]{2,1,0:T(8,128)}, f32[32,32,1]{2,1,0:T(8,128)}, u32[]{:S(2)}, u32[]{:S(2)}) collective-permute-start(f32[32,32,1]{2,1,0:T(8,128)} %broadcast.196), channel_id=1, source_target_pairs={{0,1},{1,2},{2,3},{3,0},{4,5},{5,6},{6,7},{7,4},{8,9},{9,10},{10,1... | collective-permute-start | bytes 12296 | tf_op jit(solution)/shard_map/ppermute | solution.py:28
  205.6 64.0 %collective-permute-start.25 = (f32[32,32,1]{2,1,0:T(8,128)}, f32[32,32,1]{2,1,0:T(8,128)}, u32[]{:S(2)}, u32[]{:S(2)}) collective-permute-start(f32[32,32,1]{2,1,0:T(8,128)} %broadcast.196), channel_id=1, source_target_pairs={{1,0},{2,1},{3,2},{0,3},{5,4},{6,5},{7,6},{4,7},{9,8},{10,9},{11,1... | collective-permute-start | bytes 12296 | tf_op jit(solution)/shard_map/ppermute | solution.py:29
  271.6 20.7 %collective-permute-start.28 = (f32[1,32,128]{2,1,0:T(8,128)S(1)}, f32[1,32,128]{2,1,0:T(8,128)S(1)}, u32[]{:S(2)}, u32[]{:S(2)}) collective-permute-start(f32[1,32,128]{2,1,0:T(8,128)S(1)} %get-tuple-element.81), channel_id=1, source_target_pairs={{0,16},{16,32},{32,48},{48,64},{64,80},{80,96},{96,112},{112,0},{1... | collective-permute-start | bytes 49160 | tf_op jit(solution)/shard_map/ppermute | solution.py:28
  271.6 20.7 %collective-permute-start.27 = (f32[1,32,128]{2,1,0:T(8,128)S(1)}, f32[1,32,128]{2,1,0:T(8,128)S(1)}, u32[]{:S(2)}, u32[]{:S(2)}) collective-permute-start(f32[1,32,128]{2,1,0:T(8,128)S(1)} %get-tuple-element.82), channel_id=1, source_target_pairs={{16,0},{32,16},{48,32},{64,48},{80,64},{96,80},{112,96},{0,112},{1... | collective-permute-start | bytes 49160 | tf_op jit(solution)/shard_map/ppermute | solution.py:29
  274.6 6.0 %collective-permute-start.30 = (f32[32,1,128]{2,1,0:T(1,128)S(1)}, f32[32,1,128]{2,1,0:T(1,128)S(1)}, u32[]{:S(2)}, u32[]{:S(2)}) collective-permute-start(f32[32,1,128]{2,1,0:T(1,128)S(1)} %get-tuple-element.83), channel_id=1, source_target_pairs={{0,4},{4,8},{8,12},{12,0},{1,5},{5,9},{9,13},{13,1},{2,6},{6,10},{... | collective-permute-start | bytes 49160 | tf_op jit(solution)/shard_map/ppermute | solution.py:28
  274.6 6.0 %collective-permute-start.29 = (f32[32,1,128]{2,1,0:T(1,128)S(1)}, f32[32,1,128]{2,1,0:T(1,128)S(1)}, u32[]{:S(2)}, u32[]{:S(2)}) collective-permute-start(f32[32,1,128]{2,1,0:T(1,128)S(1)} %get-tuple-element.84), channel_id=1, source_target_pairs={{4,0},{8,4},{12,8},{0,12},{5,1},{9,5},{13,9},{1,13},{6,2},{10,6},{... | collective-permute-start | bytes 49160 | tf_op jit(solution)/shard_map/ppermute | solution.py:29
  278.5 10.9 %collective-permute-start.31 = (f32[32,32,1]{2,1,0:T(8,128)S(1)}, f32[32,32,1]{2,1,0:T(8,128)S(1)}, u32[]{:S(2)}, u32[]{:S(2)}) collective-permute-start(f32[32,32,1]{2,1,0:T(8,128)S(1)} %get-tuple-element.79), channel_id=1, source_target_pairs={{1,0},{2,1},{3,2},{0,3},{5,4},{6,5},{7,6},{4,7},{9,8},{10,9},{11,1... | collective-permute-start | bytes 12296 | tf_op jit(solution)/shard_map/ppermute | solution.py:29
  280.5 11.8 %collective-permute-start.32 = (f32[32,32,1]{2,1,0:T(8,128)S(1)}, f32[32,32,1]{2,1,0:T(8,128)S(1)}, u32[]{:S(2)}, u32[]{:S(2)}) collective-permute-start(f32[32,32,1]{2,1,0:T(8,128)S(1)} %get-tuple-element.80), channel_id=1, source_target_pairs={{0,1},{1,2},{2,3},{3,0},{4,5},{5,6},{6,7},{7,4},{8,9},{9,10},{10,1... | collective-permute-start | bytes 12296 | tf_op jit(solution)/shard_map/ppermute | solution.py:28
  293.0 6.8 %collective-permute-start.36 = (f32[32,1,128]{2,1,0:T(1,128)S(1)}, f32[32,1,128]{2,1,0:T(1,128)S(1)}, u32[]{:S(2)}, u32[]{:S(2)}) collective-permute-start(f32[32,1,128]{2,1,0:T(1,128)S(1)} %get-tuple-element.77), channel_id=1, source_target_pairs={{0,4},{4,8},{8,12},{12,0},{1,5},{5,9},{9,13},{13,1},{2,6},{6,10},{... | collective-permute-start | bytes 49160 | tf_op jit(solution)/shard_map/ppermute | solution.py:28
  293.1 8.5 %collective-permute-start.35 = (f32[32,1,128]{2,1,0:T(1,128)S(1)}, f32[32,1,128]{2,1,0:T(1,128)S(1)}, u32[]{:S(2)}, u32[]{:S(2)}) collective-permute-start(f32[32,1,128]{2,1,0:T(1,128)S(1)} %get-tuple-element.78), channel_id=1, source_target_pairs={{4,0},{8,4},{12,8},{0,12},{5,1},{9,5},{13,9},{1,13},{6,2},{10,6},{... | collective-permute-start | bytes 49160 | tf_op jit(solution)/shard_map/ppermute | solution.py:29
  296.3 15.9 %collective-permute-start.34 = (f32[1,32,128]{2,1,0:T(8,128)S(1)}, f32[1,32,128]{2,1,0:T(8,128)S(1)}, u32[]{:S(2)}, u32[]{:S(2)}) collective-permute-start(f32[1,32,128]{2,1,0:T(8,128)S(1)} %get-tuple-element.75), channel_id=1, source_target_pairs={{0,16},{16,32},{32,48},{48,64},{64,80},{80,96},{96,112},{112,0},{1... | collective-permute-start | bytes 49160 | tf_op jit(solution)/shard_map/ppermute | solution.py:28
  296.3 15.9 %collective-permute-start.33 = (f32[1,32,128]{2,1,0:T(8,128)S(1)}, f32[1,32,128]{2,1,0:T(8,128)S(1)}, u32[]{:S(2)}, u32[]{:S(2)}) collective-permute-start(f32[1,32,128]{2,1,0:T(8,128)S(1)} %get-tuple-element.76), channel_id=1, source_target_pairs={{16,0},{32,16},{48,32},{64,48},{80,64},{96,80},{112,96},{0,112},{1... | collective-permute-start | bytes 49160 | tf_op jit(solution)/shard_map/ppermute | solution.py:29
  299.5 11.5 %collective-permute-start.37 = (f32[32,32,1]{2,1,0:T(8,128)S(1)}, f32[32,32,1]{2,1,0:T(8,128)S(1)}, u32[]{:S(2)}, u32[]{:S(2)}) collective-permute-start(f32[32,32,1]{2,1,0:T(8,128)S(1)} %get-tuple-element.73), channel_id=1, source_target_pairs={{1,0},{2,1},{3,2},{0,3},{5,4},{6,5},{7,6},{4,7},{9,8},{10,9},{11,1... | collective-permute-start | bytes 12296 | tf_op jit(solution)/shard_map/ppermute | solution.py:29
  299.8 12.4 %collective-permute-start.38 = (f32[32,32,1]{2,1,0:T(8,128)S(1)}, f32[32,32,1]{2,1,0:T(8,128)S(1)}, u32[]{:S(2)}, u32[]{:S(2)}) collective-permute-start(f32[32,32,1]{2,1,0:T(8,128)S(1)} %get-tuple-element.74), channel_id=1, source_target_pairs={{0,1},{1,2},{2,3},{3,0},{4,5},{5,6},{6,7},{7,4},{8,9},{9,10},{10,1... | collective-permute-start | bytes 12296 | tf_op jit(solution)/shard_map/ppermute | solution.py:28
  317.4 4.9 collective-permute-start.40
  322.6 6.2 %collective-permute-start.41 = (f32[16,16,1]{2,1,0:T(8,128)S(1)}, f32[16,16,1]{2,1,0:T(8,128)S(1)}, u32[]{:S(2)}, u32[]{:S(2)}) collective-permute-start(f32[16,16,1]{2,1,0:T(8,128)S(1)} %slice.955), channel_id=1, source_target_pairs={{0,1},{1,2},{2,3},{3,0},{4,5},{5,6},{6,7},{7,4},{8,9},{9,10},{10,1... | collective-permute-start | bytes 3080 | tf_op jit(solution)/shard_map/ppermute | solution.py:17
  343.5 5.1 collective-permute-start.42
  344.5 5.0 collective-permute-start.43
  349.5 7.1 %collective-permute-start.44 = (f32[26,5,256]{2,1,0:T(8,128)S(1)}, f32[26,5,256]{2,1,0:T(8,128)S(1)}, u32[]{:S(2)}, u32[]{:S(2)}) collective-permute-start(f32[26,5,256]{2,1,0:T(8,128)S(1)} %get-tuple-element.95), channel_id=1, source_target_pairs={{0,4},{4,8},{8,12},{12,0},{1,5},{5,9},{9,13},{13,1},{2,6},{6,10},{... | collective-permute-start | bytes 399368 | tf_op jit(solution)/shard_map/ppermute | solution.py:61
  349.6 7.0 %collective-permute-start.45 = (f32[26,5,256]{2,1,0:T(8,128)S(1)}, f32[26,5,256]{2,1,0:T(8,128)S(1)}, u32[]{:S(2)}, u32[]{:S(2)}) collective-permute-start(f32[26,5,256]{2,1,0:T(8,128)S(1)} %get-tuple-element.96), channel_id=1, source_target_pairs={{4,0},{8,4},{12,8},{0,12},{5,1},{9,5},{13,9},{1,13},{6,2},{10,6},{... | collective-permute-start | bytes 399368 | tf_op jit(solution)/shard_map/ppermute | solution.py:64
  368.9 11.4 %collective-permute-start.48 = (f32[32,32,1]{2,0,1:T(8,128)S(1)}, f32[32,32,1]{2,0,1:T(8,128)S(1)}, u32[]{:S(2)}, u32[]{:S(2)}) collective-permute-start(f32[32,32,1]{2,0,1:T(8,128)S(1)} %bitcast.48), channel_id=1, source_target_pairs={{0,3},{1,0},{2,1},{3,2},{4,7},{5,4},{6,5},{7,6},{8,11},{9,8},{10,9... | collective-permute-start | bytes 12296 | tf_op jit(solution)/shard_map/ppermute | solution.py:17
  388.8 20.9 %collective-permute-start.50 = (f32[1,32,128]{2,1,0:T(8,128)S(1)}, f32[1,32,128]{2,1,0:T(8,128)S(1)}, u32[]{:S(2)}, u32[]{:S(2)}) collective-permute-start(f32[1,32,128]{2,1,0:T(8,128)S(1)} %get-tuple-element.67), channel_id=1, source_target_pairs={{0,16},{16,32},{32,48},{48,64},{64,80},{80,96},{96,112},{112,0},{1... | collective-permute-start | bytes 49160 | tf_op jit(solution)/shard_map/ppermute | solution.py:28
  388.8 20.9 %collective-permute-start.49 = (f32[1,32,128]{2,1,0:T(8,128)S(1)}, f32[1,32,128]{2,1,0:T(8,128)S(1)}, u32[]{:S(2)}, u32[]{:S(2)}) collective-permute-start(f32[1,32,128]{2,1,0:T(8,128)S(1)} %get-tuple-element.68), channel_id=1, source_target_pairs={{16,0},{32,16},{48,32},{64,48},{80,64},{96,80},{112,96},{0,112},{1... | collective-permute-start | bytes 49160 | tf_op jit(solution)/shard_map/ppermute | solution.py:29
  391.8 5.9 %collective-permute-start.52 = (f32[32,1,128]{2,1,0:T(1,128)S(1)}, f32[32,1,128]{2,1,0:T(1,128)S(1)}, u32[]{:S(2)}, u32[]{:S(2)}) collective-permute-start(f32[32,1,128]{2,1,0:T(1,128)S(1)} %get-tuple-element.69), channel_id=1, source_target_pairs={{0,4},{4,8},{8,12},{12,0},{1,5},{5,9},{9,13},{13,1},{2,6},{6,10},{... | collective-permute-start | bytes 49160 | tf_op jit(solution)/shard_map/ppermute | solution.py:28
  391.8 5.9 %collective-permute-start.51 = (f32[32,1,128]{2,1,0:T(1,128)S(1)}, f32[32,1,128]{2,1,0:T(1,128)S(1)}, u32[]{:S(2)}, u32[]{:S(2)}) collective-permute-start(f32[32,1,128]{2,1,0:T(1,128)S(1)} %get-tuple-element.70), channel_id=1, source_target_pairs={{4,0},{8,4},{12,8},{0,12},{5,1},{9,5},{13,9},{1,13},{6,2},{10,6},{... | collective-permute-start | bytes 49160 | tf_op jit(solution)/shard_map/ppermute | solution.py:29
  395.2 11.2 %collective-permute-start.53 = (f32[32,32,1]{2,1,0:T(8,128)S(1)}, f32[32,32,1]{2,1,0:T(8,128)S(1)}, u32[]{:S(2)}, u32[]{:S(2)}) collective-permute-start(f32[32,32,1]{2,1,0:T(8,128)S(1)} %get-tuple-element.65), channel_id=1, source_target_pairs={{1,0},{2,1},{3,2},{0,3},{5,4},{6,5},{7,6},{4,7},{9,8},{10,9},{11,1... | collective-permute-start | bytes 12296 | tf_op jit(solution)/shard_map/ppermute | solution.py:29
  397.6 12.0 %collective-permute-start.54 = (f32[32,32,1]{2,1,0:T(8,128)S(1)}, f32[32,32,1]{2,1,0:T(8,128)S(1)}, u32[]{:S(2)}, u32[]{:S(2)}) collective-permute-start(f32[32,32,1]{2,1,0:T(8,128)S(1)} %get-tuple-element.66), channel_id=1, source_target_pairs={{0,1},{1,2},{2,3},{3,0},{4,5},{5,6},{6,7},{7,4},{8,9},{9,10},{10,1... | collective-permute-start | bytes 12296 | tf_op jit(solution)/shard_map/ppermute | solution.py:28
  410.4 19.5 %collective-permute-start.56 = (f32[1,32,128]{2,1,0:T(8,128)S(1)}, f32[1,32,128]{2,1,0:T(8,128)S(1)}, u32[]{:S(2)}, u32[]{:S(2)}) collective-permute-start(f32[1,32,128]{2,1,0:T(8,128)S(1)} %get-tuple-element.61), channel_id=1, source_target_pairs={{0,16},{16,32},{32,48},{48,64},{64,80},{80,96},{96,112},{112,0},{1... | collective-permute-start | bytes 49160 | tf_op jit(solution)/shard_map/ppermute | solution.py:28
  410.4 19.5 %collective-permute-start.55 = (f32[1,32,128]{2,1,0:T(8,128)S(1)}, f32[1,32,128]{2,1,0:T(8,128)S(1)}, u32[]{:S(2)}, u32[]{:S(2)}) collective-permute-start(f32[1,32,128]{2,1,0:T(8,128)S(1)} %get-tuple-element.62), channel_id=1, source_target_pairs={{16,0},{32,16},{48,32},{64,48},{80,64},{96,80},{112,96},{0,112},{1... | collective-permute-start | bytes 49160 | tf_op jit(solution)/shard_map/ppermute | solution.py:29
  413.3 4.9 collective-permute-start.58
  413.3 5.7 %collective-permute-start.57 = (f32[32,1,128]{2,1,0:T(1,128)S(1)}, f32[32,1,128]{2,1,0:T(1,128)S(1)}, u32[]{:S(2)}, u32[]{:S(2)}) collective-permute-start(f32[32,1,128]{2,1,0:T(1,128)S(1)} %get-tuple-element.64), channel_id=1, source_target_pairs={{4,0},{8,4},{12,8},{0,12},{5,1},{9,5},{13,9},{1,13},{6,2},{10,6},{... | collective-permute-start | bytes 49160 | tf_op jit(solution)/shard_map/ppermute | solution.py:29
  417.0 10.9 %collective-permute-start.59 = (f32[32,32,1]{2,1,0:T(8,128)S(1)}, f32[32,32,1]{2,1,0:T(8,128)S(1)}, u32[]{:S(2)}, u32[]{:S(2)}) collective-permute-start(f32[32,32,1]{2,1,0:T(8,128)S(1)} %get-tuple-element.59), channel_id=1, source_target_pairs={{1,0},{2,1},{3,2},{0,3},{5,4},{6,5},{7,6},{4,7},{9,8},{10,9},{11,1... | collective-permute-start | bytes 12296 | tf_op jit(solution)/shard_map/ppermute | solution.py:29
  418.3 11.6 %collective-permute-start.60 = (f32[32,32,1]{2,1,0:T(8,128)S(1)}, f32[32,32,1]{2,1,0:T(8,128)S(1)}, u32[]{:S(2)}, u32[]{:S(2)}) collective-permute-start(f32[32,32,1]{2,1,0:T(8,128)S(1)} %get-tuple-element.60), channel_id=1, source_target_pairs={{0,1},{1,2},{2,3},{3,0},{4,5},{5,6},{6,7},{7,4},{8,9},{9,10},{10,1... | collective-permute-start | bytes 12296 | tf_op jit(solution)/shard_map/ppermute | solution.py:28
  472.6 22.2 %collective-permute-start.65 = (f32[1,64,256]{2,1,0:T(8,128)S(1)}, f32[1,64,256]{2,1,0:T(8,128)S(1)}, u32[]{:S(2)}, u32[]{:S(2)}) collective-permute-start(f32[1,64,256]{2,1,0:T(8,128)S(1)} %get-tuple-element.23), channel_id=1, source_target_pairs={{0,16},{16,32},{32,48},{48,64},{64,80},{80,96},{96,112},{112,0},{1... | collective-permute-start | bytes 196616 | tf_op jit(solution)/shard_map/ppermute | solution.py:28
  472.7 22.2 %collective-permute-start.64 = (f32[1,64,256]{2,1,0:T(8,128)S(1)}, f32[1,64,256]{2,1,0:T(8,128)S(1)}, u32[]{:S(2)}, u32[]{:S(2)}) collective-permute-start(f32[1,64,256]{2,1,0:T(8,128)S(1)} %get-tuple-element.24), channel_id=1, source_target_pairs={{16,0},{32,16},{48,32},{64,48},{80,64},{96,80},{112,96},{0,112},{1... | collective-permute-start | bytes 196616 | tf_op jit(solution)/shard_map/ppermute | solution.py:29
  475.6 19.1 %collective-permute-start.67 = (f32[64,1,256]{2,1,0:T(1,128)S(1)}, f32[64,1,256]{2,1,0:T(1,128)S(1)}, u32[]{:S(2)}, u32[]{:S(2)}) collective-permute-start(f32[64,1,256]{2,1,0:T(1,128)S(1)} %get-tuple-element.25), channel_id=1, source_target_pairs={{0,4},{4,8},{8,12},{12,0},{1,5},{5,9},{9,13},{13,1},{2,6},{6,10},{... | collective-permute-start | bytes 196616 | tf_op jit(solution)/shard_map/ppermute | solution.py:28
  476.0 18.8 %collective-permute-start.66 = (f32[64,1,256]{2,1,0:T(1,128)S(1)}, f32[64,1,256]{2,1,0:T(1,128)S(1)}, u32[]{:S(2)}, u32[]{:S(2)}) collective-permute-start(f32[64,1,256]{2,1,0:T(1,128)S(1)} %get-tuple-element.26), channel_id=1, source_target_pairs={{4,0},{8,4},{12,8},{0,12},{5,1},{9,5},{13,9},{1,13},{6,2},{10,6},{... | collective-permute-start | bytes 196616 | tf_op jit(solution)/shard_map/ppermute | solution.py:29
  487.6 5.1 collective-permute-start.69
  517.0 22.0 %collective-permute-start.71 = (f32[1,64,256]{2,1,0:T(8,128)S(1)}, f32[1,64,256]{2,1,0:T(8,128)S(1)}, u32[]{:S(2)}, u32[]{:S(2)}) collective-permute-start(f32[1,64,256]{2,1,0:T(8,128)S(1)} %get-tuple-element.17), channel_id=1, source_target_pairs={{0,16},{16,32},{32,48},{48,64},{64,80},{80,96},{96,112},{112,0},{1... | collective-permute-start | bytes 196616 | tf_op jit(solution)/shard_map/ppermute | solution.py:28
  517.0 22.0 %collective-permute-start.70 = (f32[1,64,256]{2,1,0:T(8,128)S(1)}, f32[1,64,256]{2,1,0:T(8,128)S(1)}, u32[]{:S(2)}, u32[]{:S(2)}) collective-permute-start(f32[1,64,256]{2,1,0:T(8,128)S(1)} %get-tuple-element.18), channel_id=1, source_target_pairs={{16,0},{32,16},{48,32},{64,48},{80,64},{96,80},{112,96},{0,112},{1... | collective-permute-start | bytes 196616 | tf_op jit(solution)/shard_map/ppermute | solution.py:29
  519.9 18.9 %collective-permute-start.73 = (f32[64,1,256]{2,1,0:T(1,128)S(1)}, f32[64,1,256]{2,1,0:T(1,128)S(1)}, u32[]{:S(2)}, u32[]{:S(2)}) collective-permute-start(f32[64,1,256]{2,1,0:T(1,128)S(1)} %get-tuple-element.19), channel_id=1, source_target_pairs={{0,4},{4,8},{8,12},{12,0},{1,5},{5,9},{9,13},{13,1},{2,6},{6,10},{... | collective-permute-start | bytes 196616 | tf_op jit(solution)/shard_map/ppermute | solution.py:28
  520.0 18.9 %collective-permute-start.72 = (f32[64,1,256]{2,1,0:T(1,128)S(1)}, f32[64,1,256]{2,1,0:T(1,128)S(1)}, u32[]{:S(2)}, u32[]{:S(2)}) collective-permute-start(f32[64,1,256]{2,1,0:T(1,128)S(1)} %get-tuple-element.20), channel_id=1, source_target_pairs={{4,0},{8,4},{12,8},{0,12},{5,1},{9,5},{13,9},{1,13},{6,2},{10,6},{... | collective-permute-start | bytes 196616 | tf_op jit(solution)/shard_map/ppermute | solution.py:29
  531.5 5.3 collective-permute-start.75
  (17 other events, 89.1 us)
where the time goes:
time: 571 us; the launch traced here: 562 us
  local copies, waits for them, and re-layouts  151 us (26%)
  other arithmetic  148 us (26%)
  waiting for transfers between devices  122 us (21%)
  starting transfers between devices  91.6 us (16%)
  blocking collectives  47.6 us (8%)
    add x12, other arithmetic, relax_step(): centre + relax_weight * (source / (6.0 * level_scale) - centre + beside /...  93 us
    ppermute x30, starting transfers between devices, extended_2(): lax.ppermute(first, axis, [(b, a) for a, b in up])  73.6 us
    ppermute x30, waiting for transfers between devices, extended_2(): lax.ppermute(first, axis, [(b, a) for a, b in up])  49.3 us
    psum x4, blocking collectives, one_axis_at_a_time(): shard = lax.psum(shard, axis)  38.1 us
    ppermute x12, waiting for transfers between devices, passed_along(): lax.ppermute(shard, axis, [(i, (i + by) % devices) for i in range(devices)])  34.5 us
    ppermute x30, waiting for transfers between devices, extended_2(): lax.ppermute(last, axis, up)  32.1 us
    slice x4, local copies, waits for them, and re-layouts, restrict_along(): lower_side = lax.slice_in_dim(extended, 0, inner_count, 2, along)  26.1 us
    slice x4, local copies, waits for them, and re-layouts, restrict_along(): on_points = lax.slice_in_dim(extended, 1, inner_count + 1, 2, along)  25.3 us
  transfers between devices with their start and end apart: 76, of which 32 were waited for; matrix products, arithmetic and copies ran while one was open for 21% of the time, Pallas kernels for 0%

commit v1 on v0

v1 whole, which is shorter than its diff:
```python
import itertools

import jax
import jax.numpy as jnp
from jax import lax
from jax.experimental import pallas as pl
from jax.experimental.pallas import tpu as pltpu
from jax.sharding import PartitionSpec as P

F32 = jnp.float32
MESH = pl.DeviceIdType.MESH
COARSE_SWEEPS = 6
W = 0.8
C6 = W / 6.0
HIGH = lax.Precision.HIGHEST

N0, RP0 = 64, 96
PS0 = 2 * RP0
N1, H1, RP1, RO1 = 32, 4, 56, 12
PS1 = 2 * RP1
N2, H2, RP2, RO2 = 16, 8, 48, 16

XS1 = {1: (28, 5), 0: (0, 33), -1: (0, 4)}
GS1 = {1: (1, 2), 0: (0, 3), -1: (0, 1)}
XS2 = {1: (8, 8), 0: (0, 16), -1: (0, 8)}
GS2 = {1: (1, 1), 0: (0, 2), -1: (0, 1)}
PAD8 = {5: 8, 33: 40, 4: 8}
XY = [d for d in itertools.product((-1, 0, 1), repeat=2)]
XY8 = [d for d in XY if d != (0, 0)]
NEAR = [d for d in itertools.product((-1, 0, 1), repeat=3) if d != (0, 0, 0)]


def shift_weight():
    total = 0.0
    for level in range(2):
        total += 4 * W / (6.0 * 0.25**level)
    return total + COARSE_SWEEPS * W / (6.0 * 0.0625)


def make_kernel(nx, ny, nz):
    cells = float(nx * N0 * ny * N0 * nz * 256)
    far = (
        [(0, 0, k) for k in range(2, nz - 1)]
        + [(0, k, 0) for k in range(2, ny - 1)]
        + [(k, 0, 0) for k in range(2, nx - 1)]
    )
    peers = NEAR + far
    ring = {0: [(0, 0, k) for k in range(1, nz)], 1: [(0, k, 0) for k in range(1, ny)], 2: [(k, 0, 0) for k in range(1, nx)]}
    n_sem = [0]

    scratch, names = [], []

    def vm(name, *shape):
        names.append(name)
        scratch.append(pltpu.VMEM(shape, F32))

    vm("A", 66, 2, RP0, 128)
    vm("B", 67, 2, RP0, 128)
    vm("G", 64, 2, 64, 128)
    vm("PK", 4, 64, 128)
    vm("HR", 4, 2, 64, 128)
    vm("L", 1360, 256)
    vm("G1", 41, 2, RP1, 128)
    vm("WA", 41, 2, RP1, 128)
    vm("WB", 41, 2, RP1, 128)
    vm("U", 3, 40, 128)
    vm("D", 3, 40, 128)
    vm("G2", 32, RP2, 128)
    vm("VA", 33, RP2, 128)
    vm("VB", 33, RP2, 128)
    vm("PZ2", 2, 16, 128)
    vm("RZ2", 2, 4, 32, 128)
    vm("CZ1", 21, 2, 32, 128)
    vm("F1", 21, 2, RP1, 128)
    vm("CZ0", 34, 3, 48, 128)
    vm("F0", 34, 3, 80, 128)
    vm("TS", 3, 8, 128)
    vm("TR0", max(nz - 1, 1), 8, 128)
    vm("TR1", max(ny - 1, 1), 8, 128)
    vm("TR2", max(nx - 1, 1), 8, 128)
    for dx, dy in XY8:
        vm(("RT", dx, dy), XS1[dx][1], PAD8[XS1[dy][1]], 128)
        vm(("RU0", dx, dy), GS1[dx][1], PAD8[XS1[dy][1]], 128)
    for dx, dy in XY:
        vm(("RU1", dx, dy), GS1[dx][1], PAD8[XS1[dy][1]], 128)
        vm(("RD", dx, dy), GS1[dx][1], PAD8[XS1[dy][1]], 128)
    N_MSG = 4 * 6 + 34 + 26 + (nx - 1) + (ny - 1) + (nz - 1)
    scratch += [pltpu.SemaphoreType.DMA((N_MSG,)), pltpu.SemaphoreType.DMA((N_MSG,)), pltpu.SemaphoreType.DMA((8,))]

    def kernel(g_hbm, v_hbm, out_hbm, *refs):
        b = dict(zip(names, refs))
        send, recv, local = refs[len(names):]
        A, B, G = b["A"], b["B"], b["G"]
        me = (lax.axis_index("gx"), lax.axis_index("gy"), lax.axis_index("gz"))
        sizes = (nx, ny, nz)
        lane = lax.broadcasted_iota(jnp.int32, (8, 128), 1)
        l0, l127 = lane == 0, lane == 127
        zero = jnp.zeros((8, 128), F32)
        used = [0]

        def at(d):
            return tuple(lax.rem(m + (k + n), n) if k else m for m, k, n in zip(me, d, sizes))

        def post(src, dst, d):
            k = used[0]
            used[0] += 1
            c = pltpu.make_async_remote_copy(
                src_ref=src, dst_ref=dst, send_sem=send.at[k], recv_sem=recv.at[k], device_id=at(d), device_id_type=MESH
            )
            c.start()
            return c

        def flat(ref):
            s = ref.shape
            n = 1
            for k in s[:-1]:
                n *= k
            return ref.reshape(n, s[-1])

        def row(k, m=8):
            return pl.multiple_of(k, m)

        Af, Bf, Gf = flat(A), flat(B), flat(G)
        G1f, WAf, WBf = flat(b["G1"]), flat(b["WA"]), flat(b["WB"])

        def clear(ref):
            f = flat(ref)
            n = f.shape[0] // 8
            per = 1
            for k in range(16, 0, -1):
                if n % k == 0:
                    per = k
                    break

            def step(i, _):
                for k in range(per):
                    f[pl.ds(row((i * per + k) * 8), 8)] = zero
                return 0

            lax.fori_loop(0, n // per, step, 0)

        barrier = pltpu.get_barrier_semaphore()
        for d in peers:
            pl.semaphore_signal(barrier, inc=1, device_id=at(d), device_id_type=MESH)
        loads = []
        for t in range(2):
            loads.append(pltpu.make_async_copy(v_hbm.at[:, :, t * 128 : t * 128 + 128], A.at[1:65, t, 8:72, :], local.at[t]))
            loads.append(pltpu.make_async_copy(g_hbm.at[:, :, t * 128 : t * 128 + 128], G.at[:, t, :, :], local.at[2 + t]))
        for k in (0, 2, 1, 3):
            loads[k].start()
        for name in names:
            if isinstance(name, tuple):
                clear(b[name])
        clear(b["G1"])
        for dst in (B.at[0], B.at[65], B.at[66]):
            clear(dst)

        def clear_rows(i, _):
            for t in range(2):
                Bf[pl.ds(row(i * PS0 + t * RP0), 8)] = zero
                for r in (72, 80, 88):
                    Bf[pl.ds(row(i * PS0 + t * RP0 + r), 8)] = zero
            return 0

        lax.fori_loop(1, 65, clear_rows, 0)
        pl.semaphore_wait(barrier, len(peers))
        loads[0].wait()
        loads[2].wait()

        half = jnp.bitwise_and(lane + 1, 127) // 2

        def put_face(pack, x, yt, first, last):
            both = pltpu.roll(jnp.where(l0, first, last), jnp.bitwise_and(2 * x, 127), 1)
            r = pl.ds(yt * 8, 8)
            pack[r] = jnp.where(half == x, both, pack[r])

        def pack_first(i, _):
            for yt in range(8):
                keep = b["PK"][0, yt * 8 : yt * 8 + 8]
                for p in range(4):
                    x = i * 4 + p
                    r = row((x + 1) * PS0 + 8 + yt * 8)
                    both = pltpu.roll(
                        jnp.where(l0, Af[pl.ds(r, 8)], Af[pl.ds(r + RP0, 8)]), jnp.bitwise_and(2 * x, 127), 1
                    )
                    keep = jnp.where(half == x, both, keep)
                b["PK"][0, yt * 8 : yt * 8 + 8] = keep
            return 0

        lax.fori_loop(0, 16, pack_first, 0)

        def faces(V, k):
            pk = b["PK"].at[k]
            return [
                post(V.at[64, :, 8:72, :], V.at[0, :, 8:72, :], (1, 0, 0)),
                post(V.at[1, :, 8:72, :], V.at[65, :, 8:72, :], (-1, 0, 0)),
                post(V.at[1:65, :, 71:72, :], V.at[1:65, :, 7:8, :], (0, 1, 0)),
                post(V.at[1:65, :, 8:9, :], V.at[1:65, :, 72:73, :], (0, -1, 0)),
                post(pk, b["HR"].at[k, 0], (0, 0, 1)),
                post(pk, b["HR"].at[k, 1], (0, 0, -1)),
            ]

        odd = jnp.bitwise_and(lane, 1) == 1

        def merge(k):
            for yt in range(8):
                r = slice(yt * 8, yt * 8 + 8)
                b["HR"][k, 0, r] = jnp.where(odd, b["HR"][k, 0, r], b["HR"][k, 1, r])

        def stencil(Vf, k, op, emit, carry=0):
            summed = isinstance(carry, tuple)

            def step(i, carry):
                base = row((i * 4 + 1) * PS0)
                for yt in range(8):
                    o = 8 + yt * 8
                    c = {
                        (p, t): Vf[pl.ds(row(base + (p * PS0 + t * RP0 + o)), 8)] for p in range(-1, 5) for t in range(2)
                    }
                    h = b["HR"][k, 0, yt * 8 : yt * 8 + 8]
                    outs = []
                    for p in range(4):
                        x = i * 4 + p
                        e = pltpu.roll(h, jnp.bitwise_and(128 - 2 * x, 127), 1)
                        c0, c1 = c[p, 0], c[p, 1]
                        zs = (
                            pltpu.roll(jnp.where(l127, e, c0), 1, 1) + pltpu.roll(jnp.where(l0, c1, c0), 127, 1),
                            pltpu.roll(jnp.where(l127, c0, c1), 1, 1) + pltpu.roll(jnp.where(l0, e, c1), 127, 1),
                        )
                        res = []
                        for t in range(2):
                            q = base + (p * PS0 + t * RP0 + o)
                            ys = Vf[pl.ds(q - 1, 8)] + Vf[pl.ds(q + 1, 8)]
                            beside = (c[p - 1, t] + c[p + 1, t]) + ys + zs[t]
                            g = Gf[pl.ds(row(x * 128 + t * 64 + yt * 8), 8)]
                            res.append(op(c[p, t], beside, g))
                            if summed:
                                carry = (carry[0] + c[p, t], carry[1] + g)
                        outs.append((x, res))
                    emit(i, yt, outs)
                return carry

            return lax.fori_loop(0, 16, step, carry)

        def relax0(c, beside, g):
            return (1.0 - W) * c + C6 * (beside + g)

        def defect0(c, beside, g):
            return g - 6.0 * c + beside

        def storing(Df, k):
            def emit(i, yt, outs):
                for x, res in outs:
                    for t in range(2):
                        Df[pl.ds(row((x + 1) * PS0 + t * RP0 + 8 + yt * 8), 8)] = res[t]
                if k is not None:
                    keep = b["PK"][k, yt * 8 : yt * 8 + 8]
                    for x, res in outs:
                        both = pltpu.roll(jnp.where(l0, res[0], res[1]), jnp.bitwise_and(2 * x, 127), 1)
                        keep = jnp.where(half == x, both, keep)
                    b["PK"][k, yt * 8 : yt * 8 + 8] = keep

            return emit

        def total_stage(stage, tile):
            b["TS"][stage] = tile
            rec = b[f"TR{stage}"]
            return [post(b["TS"].at[stage], rec.at[j], d) for j, d in enumerate(ring[stage])]

        def total_wait(stage, msgs):
            tile = b["TS"][stage]
            for j, m in enumerate(msgs):
                m.wait()
                tile = tile + b[f"TR{stage}"][j]
            return tile

        msgs = faces(A, 0)
        loads[1].wait()
        loads[3].wait()
        for m in msgs:
            m.wait()
        merge(0)
        sums = stencil(Af, 0, relax0, storing(Bf, 1), (zero, zero))
        msgs = faces(B, 1)
        sum_msgs = total_stage(0, sums[0] + shift_weight() * sums[1])
        for m in msgs:
            m.wait()
        merge(1)
        stencil(Bf, 1, relax0, storing(Af, 2))
        msgs = faces(A, 2)
        sum_msgs = total_stage(1, total_wait(0, sum_msgs))
        for m in msgs:
            m.wait()
        merge(2)

        stencil(Af, 2, defect0, storing(Bf, None))

        def clear_rims(i, _):
            for t in range(2):
                Bf[pl.ds(i * PS0 + t * RP0 + 7, 1)] = zero[0:1]
                Bf[pl.ds(i * PS0 + t * RP0 + 72, 1)] = zero[0:1]
            return 0

        lax.fori_loop(1, 65, clear_rims, 0)
        for dst in (B.at[0], B.at[65]):
            clear(dst)
        L = b["L"]

        def restrict_xy(Df, plane, slab, start):
            rows = []
            for dp in range(3):
                q = plane + dp * slab + start
                lo, on, up = (Df[pl.ds(q + k, 8, stride=2)] for k in range(3))
                rows.append(0.25 * (lo + up) + 0.5 * on)
            return 0.25 * (rows[0] + rows[2]) + 0.5 * rows[1]

        def restrict0(i, _):
            for t in range(2):
                for ct in range(5):
                    L[pl.ds(row(i * 40 + ct * 8), 8), t * 128 : t * 128 + 128] = restrict_xy(
                        Bf, i * 2 * PS0, PS0, t * RP0 + 7 + 16 * ct
                    )
            return 0

        lax.fori_loop(0, 33, restrict0, 0)

        def grid(rows, cols):
            return (
                lax.broadcasted_iota(jnp.int32, (rows, cols), 0),
                lax.broadcasted_iota(jnp.int32, (rows, cols), 1),
            )

        f, c = grid(256, 256)
        gap = jnp.abs(f - 2 * c)
        R0 = jnp.where(gap == 0, 0.5, jnp.where(gap == 1, 0.25, 0.0)).astype(F32)

        def rz0(i, _):
            res = jnp.dot(L[pl.ds(row(i * 440), 440), :], R0, precision=HIGH, preferred_element_type=F32)
            for p in range(11):
                for t in range(2):
                    for ct in range(5):
                        G1f[pl.ds((i * 11 + (p + H1)) * PS1 + (t * RP1 + RO1 + ct * 8), 8)] = res[
                            p * 40 + ct * 8 : p * 40 + ct * 8 + 8, t * 128 : t * 128 + 128
                        ]
            return 0

        lax.fori_loop(0, 3, rz0, 0)

        Uf, Df_ = flat(b["U"]), flat(b["D"])
        for name in ("U", "D"):
            clear(b[name])
        slot8 = lane // 8

        def pack1(x, _):
            grp, j = x // 16, jnp.bitwise_and(x, 15)
            for ct in range(5):
                q = (x + H1) * PS1 + RO1 + ct * 8
                t0, e = G1f[pl.ds(q, 8)], G1f[pl.ds(q + RP1, 8)]
                r = pl.ds(row(grp * 40 + ct * 8), 8)
                Uf[r] = jnp.where(slot8 == j, pltpu.roll(jnp.where(l0, e, t0), jnp.bitwise_and(4 + 8 * j, 127), 1), Uf[r])
                Df_[r] = jnp.where(slot8 == j, pltpu.roll(t0, 8 * j, 1), Df_[r])
            return 0

        lax.fori_loop(0, 33, pack1, 0)
        G1 = b["G1"]
        msgs1 = []

        def along(spec, k, off=0):
            return slice(spec[k][0] + off, spec[k][0] + off + spec[k][1])

        for dx, dy in XY:
            n = XS1[dy][1]
            ys = along(XS1, dy)
            gs = along(GS1, dx)
            if (dx, dy) != (0, 0):
                msgs1.append(
                    post(G1.at[along(XS1, dx, H1), 0, along(XS1, dy, RO1), :], b["RT", dx, dy].at[:, 0:n, :], (dx, dy, 0))
                )
                msgs1.append(post(b["U"].at[gs, ys, :], b["RU0", dx, dy].at[:, 0:n, :], (dx, dy, 0)))
            msgs1.append(post(b["U"].at[gs, ys, :], b["RU1", dx, dy].at[:, 0:n, :], (dx, dy, 1)))
            msgs1.append(post(b["D"].at[gs, ys, :], b["RD", dx, dy].at[:, 0:n, :], (dx, dy, -1)))
        sum_msgs = total_stage(2, total_wait(1, sum_msgs))
        for m in msgs1:
            m.wait()

        def add1(q, v):
            G1f[pl.ds(q, 8)] = G1f[pl.ds(q, 8)] + v

        for dx, dy in XY:
            sx, n = XS1[dx]
            sy = XS1[dy][0]
            tiles = PAD8[XS1[dy][1]] // 8
            g0 = GS1[dx][0]

            def unpack(k, _, dx=dx, dy=dy, sx=sx, sy=sy, tiles=tiles, g0=g0):
                s = k + sx
                grp, j = s // 16 - g0, jnp.bitwise_and(s, 15)
                for ct in range(tiles):
                    q = (k + (sx - N1 * dx + H1)) * PS1 + (sy - N1 * dy + RO1 + ct * 8)
                    up = jnp.bitwise_and(124 - 8 * j, 127)
                    u1 = pltpu.roll(b["RU1", dx, dy][grp, ct * 8 : ct * 8 + 8], up, 1)
                    dn = pltpu.roll(b["RD", dx, dy][grp, ct * 8 : ct * 8 + 8], jnp.bitwise_and(128 - 8 * j, 127), 1)
                    e = jnp.where(lane >= 124, u1, 0.0) + jnp.where(lane < 4, dn, 0.0)
                    t0 = jnp.where(l0, u1, 0.0)
                    if (dx, dy) != (0, 0):
                        u0 = pltpu.roll(b["RU0", dx, dy][grp, ct * 8 : ct * 8 + 8], up, 1)
                        e = e + jnp.where(l0, u0, 0.0)
                        t0 = t0 + b["RT", dx, dy][k, ct * 8 : ct * 8 + 8]
                    add1(q, t0)
                    add1(q + RP1, e)
                return 0

            lax.fori_loop(0, n, unpack, 0)

        def ring1(Vf, op, emit, lo, hi):
            def step(x, _):
                for ct in range(5):
                    q = row(x * PS1 + 8 + ct * 8)
                    c = (Vf[pl.ds(q, 8)], Vf[pl.ds(q + RP1, 8)])
                    for t in range(2):
                        a, o = c[t], c[1 - t]
                        zs = pltpu.roll(jnp.where(l127, o, a), 1, 1) + pltpu.roll(jnp.where(l0, o, a), 127, 1)
                        s = q + t * RP1
                        beside = (
                            (Vf[pl.ds(s - PS1, 8)] + Vf[pl.ds(s + PS1, 8)]) + (Vf[pl.ds(s - 1, 8)] + Vf[pl.ds(s + 1, 8)]) + zs
                        )
                        emit(x, t, ct, s, op(a, beside, G1f[pl.ds(s, 8)]))
                return 0

            lax.fori_loop(lo + H1, hi + H1, step, 0)

        first = W / (6.0 * 0.25)

        def put1(Df):
            def emit(x, t, ct, s, v):
                Df[pl.ds(s, 8)] = v

            return emit

        ring1(G1f, lambda a, beside, g: ((2.0 - W) * first) * a + (C6 * first) * beside, put1(WAf), -3, 35)
        ring1(WAf, lambda a, beside, g: g - 0.25 * (6.0 * a - beside), put1(WBf), -1, 32)

        def restrict1(i, _):
            for t in range(2):
                for ct in range(2):
                    L[pl.ds(row(i * 16 + ct * 8), 8), t * 128 : t * 128 + 128] = restrict_xy(
                        WBf, (2 * i + (H1 - 1)) * PS1, PS1, t * RP1 + RO1 - 1 + 16 * ct
                    )
            return 0

        lax.fori_loop(0, 16, restrict1, 0)
        f, c = grid(256, 128)
        gap = jnp.abs(jnp.where(f < 192, f, f - 256) - 2 * c)
        R1 = jnp.where(c < 64, jnp.where(gap == 0, 0.5, jnp.where(gap == 1, 0.25, 0.0)), 0.0).astype(F32)
        G2, VA, VB = b["G2"], b["VA"], b["VB"]
        G2f, VAf, VBf = flat(G2), flat(VA), flat(VB)
        res = jnp.dot(L[0:256, :], R1, precision=HIGH, preferred_element_type=F32)
        slot16 = lane // 16
        for x in range(16):
            for ct in range(2):
                G2[x + H2, RO2 + ct * 8 : RO2 + ct * 8 + 8] = res[x * 16 + ct * 8 : x * 16 + ct * 8 + 8]
        for grp in range(2):
            for ct in range(2):
                acc = zero
                for j in range(8):
                    v = res[(grp * 8 + j) * 16 + ct * 8 : (grp * 8 + j) * 16 + ct * 8 + 8]
                    v = jnp.where(lane < 8, v, pltpu.roll(v, 128 - 48, 1))
                    acc = jnp.where(slot16 == j, pltpu.roll(v, 16 * j, 1) if j else v, acc)
                b["PZ2"][grp, ct * 8 : ct * 8 + 8] = acc
        msgs2 = []
        for dx, dy in XY:
            px, py = along(XS2, dx), along(XS2, dy)
            if (dx, dy) != (0, 0):
                msgs2.append(
                    post(
                        G2.at[along(XS2, dx, H2), along(XS2, dy, RO2), :],
                        G2.at[along(XS2, dx, H2 - N2 * dx), along(XS2, dy, RO2 - N2 * dy), :],
                        (dx, dy, 0),
                    )
                )
            gs = along(GS2, dx)
            gd = along(GS2, dx, 1 - 2 * dx)
            yd = along(XS2, dy, 8 - N2 * dy)
            for side, dz in ((0, 1), (1, -1)):
                msgs2.append(post(b["PZ2"].at[gs, py, :], b["RZ2"].at[side, gd, yd, :], (dx, dy, dz)))
        for m in msgs2:
            m.wait()

        first2 = W / (6.0 * 0.0625)

        def spread(grp, _):
            for ct in range(4):
                m = jnp.where(
                    jnp.bitwise_and(lane, 15) < 8,
                    b["RZ2"][1, grp, ct * 8 : ct * 8 + 8],
                    b["RZ2"][0, grp, ct * 8 : ct * 8 + 8],
                )
                for j in range(8):
                    hi = pltpu.roll(m, (64 - 16 * j) % 128, 1)
                    lo = pltpu.roll(m, 112 - 16 * j, 1) if j < 7 else m
                    r = pl.ds(row((grp * 8 + j) * RP2 + 8 + ct * 8), 8)
                    own = G2f[r]
                    v = jnp.where(lane < 64, own, jnp.where(lane < 72, hi, jnp.where(lane >= 120, lo, 0.0)))
                    G2f[r] = v
                    VAf[r] = first2 * v
            return 0

        lax.fori_loop(0, 4, spread, 0)

        def coarse(Sf, Tf, lo, hi):
            def step(k, _):
                for ct in range(4):
                    q = row(k * RP2 + 8 + ct * 8)
                    a = Sf[pl.ds(q, 8)]
                    beside = (
                        (Sf[pl.ds(q - RP2, 8)] + Sf[pl.ds(q + RP2, 8)])
                        + (Sf[pl.ds(q - 1, 8)] + Sf[pl.ds(q + 1, 8)])
                        + (pltpu.roll(a, 1, 1) + pltpu.roll(a, 127, 1))
                    )
                    Tf[pl.ds(q, 8)] = (1.0 - W) * a + (C6 * beside + first2 * G2f[pl.ds(q, 8)])
                return 0

            lax.fori_loop(lo, hi, step, 0)

        src, dst = VAf, VBf
        for k in range(COARSE_SWEEPS - 1):
            coarse(src, dst, 2 + k, 31 - k)
            src, dst = dst, src

        f, c = grid(128, 256)
        gap = jnp.abs(jnp.where(c < 192, c, c - 256) - 2 * jnp.where(f < 96, f, f - 128))
        P1 = jnp.where(gap == 0, 1.0, jnp.where(gap == 1, 0.5, 0.0)).astype(F32)
        CZ1f, F1f = flat(b["CZ1"]), flat(b["F1"])
        for k in range(20):
            L[k * 24 : k * 24 + 24, 0:128] = src[pl.ds((k + 6) * RP2 + 12, 24)]
        res = jnp.dot(L[0:480, 0:128], P1, precision=HIGH, preferred_element_type=F32)
        for k in range(20):
            for t in range(2):
                b["CZ1"][k, t, 0:24] = res[k * 24 : k * 24 + 24, t * 128 : t * 128 + 128]

        def widen1(k, _):
            for t in range(2):
                for ct in range(3):
                    q = k * 64 + (t * 32 + ct * 8)
                    v, n = CZ1f[pl.ds(q, 8)], CZ1f[pl.ds(q + 1, 8)]
                    o = k * PS1 + (t * RP1 + 4 + 16 * ct)
                    F1f[pl.ds(o, 8, stride=2)] = v
                    F1f[pl.ds(o + 1, 8, stride=2)] = 0.5 * (v + n)
            return 0

        lax.fori_loop(0, 20, widen1, 0)

        def correct1(k, _):
            for t in range(2):
                for ct in range(5):
                    o = t * RP1 + 8 + ct * 8
                    v = F1f[pl.ds(row(k * PS1 + o), 8)]
                    n = F1f[pl.ds(row((k + 1) * PS1 + o), 8)]
                    q = row(2 * k * PS1 + o)
                    WAf[pl.ds(q, 8)] = WAf[pl.ds(q, 8)] + v
                    q = row((2 * k + 1) * PS1 + o)
                    WAf[pl.ds(q, 8)] = WAf[pl.ds(q, 8)] + 0.5 * (v + n)
            return 0

        lax.fori_loop(0, 20, correct1, 0)

        def relax1(a, beside, g):
            return (1.0 - W) * a + (C6 * beside + first * g)

        def put_l(x, t, ct, s, v):
            L[pl.ds(row((x - (H1 - 1)) * 40 + ct * 8), 8), t * 128 : t * 128 + 128] = v

        ring1(WAf, relax1, put1(WBf), -2, 34)
        ring1(WBf, relax1, put_l, -1, 33)

        f, c = grid(256, 384)
        gap = jnp.abs(jnp.where(c <= 256, c, jnp.where(c == 383, -1, 9999)) - 2 * jnp.where(f < 192, f, f - 256))
        P0 = jnp.where(gap == 0, 1.0, jnp.where(gap == 1, 0.5, 0.0)).astype(F32)
        CZ0f, F0f = flat(b["CZ0"]), flat(b["F0"])

        def pz0(i, _):
            res = jnp.dot(L[pl.ds(row(i * 680), 680), :], P0, precision=HIGH, preferred_element_type=F32)
            for p in range(17):
                for t in range(3):
                    CZ0f[pl.ds(row((i * 17 + p) * 144 + t * 48), 40)] = res[p * 40 : p * 40 + 40, t * 128 : t * 128 + 128]
            return 0

        lax.fori_loop(0, 2, pz0, 0)

        def widen0(k, _):
            for t in range(3):
                for ct in range(5):
                    q = k * 144 + (t * 48 + ct * 8)
                    v, n = CZ0f[pl.ds(q, 8)], CZ0f[pl.ds(q + 1, 8)]
                    o = k * 240 + (t * 80 + 16 * ct)
                    F0f[pl.ds(o, 8, stride=2)] = v
                    F0f[pl.ds(o + 1, 8, stride=2)] = 0.5 * (v + n)
            return 0

        lax.fori_loop(0, 34, widen0, 0)

        def add0(plane, t, r, v):
            q = pl.ds(row(plane * PS0 + t * RP0 + r), 8)
            Af[q] = Af[q] + v

        def get0(k, t, r):
            return F0f[pl.ds(row(k * 240 + t * 80 + r), 8)]

        for t in range(2):
            for r in range(8, 72, 8):
                add0(0, t, r, 0.5 * (get0(0, t, r) + get0(1, t, r)))
                add0(65, t, r, get0(33, t, r))

        def correct0(i, _):
            for t in range(2):
                for r in range(0, 80, 8):
                    v, n = get0(i + 1, t, r), get0(i + 2, t, r)
                    add0(2 * i + 1, t, r, v)
                    add0(2 * i + 2, t, r, 0.5 * (v + n))
            for yt in range(8):
                v, n = get0(i + 1, 2, 8 + yt * 8), get0(i + 2, 2, 8 + yt * 8)
                h = b["HR"][2, 0, yt * 8 : yt * 8 + 8]
                for x, w in ((2 * i, v), (2 * i + 1, 0.5 * (v + n))):
                    h = h + jnp.where(half == x, pltpu.roll(w, jnp.bitwise_and(2 * x, 127), 1), 0.0)
                b["HR"][2, 0, yt * 8 : yt * 8 + 8] = h
            return 0

        lax.fori_loop(0, 32, correct0, 0)

        stencil(Af, 2, relax0, storing(Bf, 3))
        msgs = faces(B, 3)
        tile = total_wait(2, sum_msgs)
        mean = jnp.sum(tile, keepdims=True) / cells
        mean = jnp.broadcast_to(mean, (8, 128))
        for m in msgs:
            m.wait()
        merge(3)
        stencil(Bf, 3, lambda c, beside, g: relax0(c, beside, g) - mean, storing(Af, None))
        outs = []
        for t in range(2):
            outs.append(pltpu.make_async_copy(A.at[1:65, t, 8:72, :], out_hbm.at[:, :, t * 128 : t * 128 + 128], local.at[4 + t]))
        for o in outs:
            o.start()
        for o in outs:
            o.wait()

    return kernel, scratch


def solution(mesh):
    nx, ny, nz = (mesh.shape[a] for a in ("gx", "gy", "gz"))
    kernel, scratch = make_kernel(nx, ny, nz)

    def shards(right_side, initial_guess):
        assert right_side.shape == (64, 64, 256)
        return pl.pallas_call(
            kernel,
            out_shape=jax.ShapeDtypeStruct(right_side.shape, F32),
            in_specs=[pl.BlockSpec(memory_space=pl.ANY)] * 2,
            out_specs=pl.BlockSpec(memory_space=pl.ANY),
            scratch_shapes=scratch,
            compiler_params=pltpu.CompilerParams(collective_id=0, has_side_effects=True, vmem_limit_bytes=60 << 20),
        )(right_side, initial_guess)

    placed = P("gx", "gy", "gz")
    return jax.shard_map(shards, mesh=mesh, in_specs=(placed, placed), out_specs=placed, check_vma=False)
```

time: 571 us -> 142 us (0.25); the launches traced: 562 us -> 141 us
  other arithmetic: 148 us -> 0 us
  local copies, waits for them, and re-layouts: 151 us -> 4.7 us
  Pallas kernels: 0 us -> 137 us
  waiting for transfers between devices: 122 us -> 0 us
  starting transfers between devices: 91.6 us -> 0 us
  blocking collectives: 47.6 us -> 0 us
    pallas_call x0 -> x1, Pallas kernels: none -> 137 us  [shards(): pl.pallas_call(kernel, out_shape=jax.ShapeDtypeStruct(right_side.shape, F...]
    ppermute x76 -> x0, waiting for transfers between devices: 122 us -> none  [the longest x30 49.3 us: extended_2(): lax.ppermute(first, axis, [(b, a) for a, b in up])]
    slice x78 -> x0, local copies, waits for them, and re-layouts: 104 us -> none  [the longest x4 26.1 us: restrict_along(): lower_side = lax.slice_in_dim(extended, 0, inner_count, 2, along)]
    add x20 -> x0, other arithmetic: 101 us -> none  [the longest x12 93 us: relax_step(): centre + relax_weight * (source / (6.0 * level_scale) - centre + beside /...]
    ppermute x76 -> x0, starting transfers between devices: 91.6 us -> none  [the longest x30 73.6 us: extended_2(): lax.ppermute(first, axis, [(b, a) for a, b in up])]
    psum x4 -> x0, blocking collectives: 38.1 us -> none  [one_axis_at_a_time(): shard = lax.psum(shard, axis)]
    sub x3 -> x0, other arithmetic: 24.8 us -> none  [the longest x2 22.3 us: defect_of(): return source - level_scale * (6.0 * centre - beside)]
    another operation x8 -> x0, local copies, waits for them, and re-layouts: 14.6 us -> none  [the longest x5 13.7 us: prolong_along(): stacked = jnp.stack([values, between], along + 1)]
  transfers between devices with their start and end apart: 76 -> 0, of which waited for: 32 -> 0; matrix products, arithmetic and copies ran while one was open for 21% -> 0% of each run, Pallas kernels for 0% -> 0%
where the time goes in v1:
time: 142 us; the launch traced here: 141 us
  Pallas kernels  137 us (96%)
  local copies, waits for them, and re-layouts  4.7 us (3%)
    pallas_call x1, Pallas kernels, shards(): pl.pallas_call(kernel, out_shape=jax.ShapeDtypeStruct(right_side.shape, F...  137 us
    unnamed x1, local copies, waits for them, and re-layouts  4.7 us

profile of v1, /device:TPU:0, one launch (start us, length us, event | category | flops | bytes accessed | tf_op | source)
XLA Modules:
  0.0 141.4 jit_solution(6277982602160157480)
XLA Ops:
  0.0 136.7 %shard_map.28 = f32[64,64,256]{2,1,0:T(8,128)} custom-call(f32[64,64,256]{2,1,0:T(8,128)} %g_hbm.1, f32[64,64,256]{2,1,0:T(8,128)} %v_hbm.1), custom_call_target="tpu_custom_call" | custom-call | tf_op jit(solution)/shard_map/pallas_call | solution.py:656
  136.7 4.7 %copy.4 = f32[64,64,256]{2,1,0:T(8,128)} copy(f32[64,64,256]{2,1,0:T(8,128)} %shard_map.28) | data formatting | bytes 8388608

commit v2 on v1

--- a/solution.py
+++ b/solution.py
@@ -169,26 +169,6 @@
 
         half = jnp.bitwise_and(lane + 1, 127) // 2
 
-        def put_face(pack, x, yt, first, last):
-            both = pltpu.roll(jnp.where(l0, first, last), jnp.bitwise_and(2 * x, 127), 1)
-            r = pl.ds(yt * 8, 8)
-            pack[r] = jnp.where(half == x, both, pack[r])
-
-        def pack_first(i, _):
-            for yt in range(8):
-                keep = b["PK"][0, yt * 8 : yt * 8 + 8]
-                for p in range(4):
-                    x = i * 4 + p
-                    r = row((x + 1) * PS0 + 8 + yt * 8)
-                    both = pltpu.roll(
-                        jnp.where(l0, Af[pl.ds(r, 8)], Af[pl.ds(r + RP0, 8)]), jnp.bitwise_and(2 * x, 127), 1
-                    )
-                    keep = jnp.where(half == x, both, keep)
-                b["PK"][0, yt * 8 : yt * 8 + 8] = keep
-            return 0
-
-        lax.fori_loop(0, 16, pack_first, 0)
-
         def faces(V, k):
             pk = b["PK"].at[k]
             return [
@@ -205,62 +185,61 @@
         def merge(k):
             for yt in range(8):
                 r = slice(yt * 8, yt * 8 + 8)
-                b["HR"][k, 0, r] = jnp.where(odd, b["HR"][k, 0, r], b["HR"][k, 1, r])
-
-        def stencil(Vf, k, op, emit, carry=0):
+                b["HR"][k, 0, r] = jnp.where(odd, pltpu.roll(b["HR"][k, 1, r], 127, 1), pltpu.roll(b["HR"][k, 0, r], 1, 1))
+
+        def put_faces(Df, k, i):
+            for yt in range(8):
+                keep = b["PK"][k, yt * 8 : yt * 8 + 8]
+                for p in range(4):
+                    x = i * 4 + p
+                    r = row((i * 4 + 1) * PS0) + (p * PS0 + 8 + yt * 8)
+                    both = jnp.where(l0, Df[pl.ds(r, 8)], Df[pl.ds(r + RP0, 8)])
+                    both = pltpu.roll(both, jnp.bitwise_and(2 * x, 127), 1)
+                    keep = jnp.where(half == x, both, keep)
+                b["PK"][k, yt * 8 : yt * 8 + 8] = keep
+
+        def stencil(Vf, Df, k, op, faces_to=None, carry=0):
             summed = isinstance(carry, tuple)
 
             def step(i, carry):
                 base = row((i * 4 + 1) * PS0)
+                if faces_to is not None:
+                    put_faces(Df, faces_to, jnp.maximum(i - 1, 0))
                 for yt in range(8):
                     o = 8 + yt * 8
                     c = {
                         (p, t): Vf[pl.ds(row(base + (p * PS0 + t * RP0 + o)), 8)] for p in range(-1, 5) for t in range(2)
                     }
                     h = b["HR"][k, 0, yt * 8 : yt * 8 + 8]
-                    outs = []
                     for p in range(4):
                         x = i * 4 + p
                         e = pltpu.roll(h, jnp.bitwise_and(128 - 2 * x, 127), 1)
                         c0, c1 = c[p, 0], c[p, 1]
+                        up0, up1, dn0, dn1 = (pltpu.roll(v, n, 1) for n in (1, 127) for v in (c0, c1))
                         zs = (
-                            pltpu.roll(jnp.where(l127, e, c0), 1, 1) + pltpu.roll(jnp.where(l0, c1, c0), 127, 1),
-                            pltpu.roll(jnp.where(l127, c0, c1), 1, 1) + pltpu.roll(jnp.where(l0, e, c1), 127, 1),
+                            jnp.where(l0, e, up0) + jnp.where(l127, dn1, dn0),
+                            jnp.where(l0, up0, up1) + jnp.where(l127, e, dn1),
                         )
-                        res = []
                         for t in range(2):
                             q = base + (p * PS0 + t * RP0 + o)
                             ys = Vf[pl.ds(q - 1, 8)] + Vf[pl.ds(q + 1, 8)]
                             beside = (c[p - 1, t] + c[p + 1, t]) + ys + zs[t]
                             g = Gf[pl.ds(row(x * 128 + t * 64 + yt * 8), 8)]
-                            res.append(op(c[p, t], beside, g))
+                            Df[pl.ds(row(q), 8)] = op(c[p, t], beside, g)
                             if summed:
                                 carry = (carry[0] + c[p, t], carry[1] + g)
-                        outs.append((x, res))
-                    emit(i, yt, outs)
                 return carry
 
-            return lax.fori_loop(0, 16, step, carry)
+            carry = lax.fori_loop(0, 16, step, carry)
+            if faces_to is not None:
+                put_faces(Df, faces_to, 15)
+            return carry
 
         def relax0(c, beside, g):
             return (1.0 - W) * c + C6 * (beside + g)
 
         def defect0(c, beside, g):
             return g - 6.0 * c + beside
-
-        def storing(Df, k):
-            def emit(i, yt, outs):
-                for x, res in outs:
-                    for t in range(2):
-                        Df[pl.ds(row((x + 1) * PS0 + t * RP0 + 8 + yt * 8), 8)] = res[t]
-                if k is not None:
-                    keep = b["PK"][k, yt * 8 : yt * 8 + 8]
-                    for x, res in outs:
-                        both = pltpu.roll(jnp.where(l0, res[0], res[1]), jnp.bitwise_and(2 * x, 127), 1)
-                        keep = jnp.where(half == x, both, keep)
-                    b["PK"][k, yt * 8 : yt * 8 + 8] = keep
-
-            return emit
 
         def total_stage(stage, tile):
             b["TS"][stage] = tile
@@ -274,26 +253,32 @@
                 tile = tile + b[f"TR{stage}"][j]
             return tile
 
+        def pack_first(i, _):
+            put_faces(Af, 0, 2 * i)
+            put_faces(Af, 0, 2 * i + 1)
+            return 0
+
+        lax.fori_loop(0, 8, pack_first, 0)
         msgs = faces(A, 0)
         loads[1].wait()
         loads[3].wait()
         for m in msgs:
             m.wait()
         merge(0)
-        sums = stencil(Af, 0, relax0, storing(Bf, 1), (zero, zero))
+        sums = stencil(Af, Bf, 0, relax0, 1, (zero, zero))
         msgs = faces(B, 1)
         sum_msgs = total_stage(0, sums[0] + shift_weight() * sums[1])
         for m in msgs:
             m.wait()
         merge(1)
-        stencil(Bf, 1, relax0, storing(Af, 2))
+        stencil(Bf, Af, 1, relax0, 2)
         msgs = faces(A, 2)
         sum_msgs = total_stage(1, total_wait(0, sum_msgs))
         for m in msgs:
             m.wait()
         merge(2)
 
-        stencil(Af, 2, defect0, storing(Bf, None))
+        stencil(Af, Bf, 2, defect0)
 
         def clear_rims(i, _):
             for t in range(2):
@@ -346,22 +331,17 @@
 
         lax.fori_loop(0, 3, rz0, 0)
 
-        Uf, Df_ = flat(b["U"]), flat(b["D"])
-        for name in ("U", "D"):
-            clear(b[name])
         slot8 = lane // 8
-
-        def pack1(x, _):
-            grp, j = x // 16, jnp.bitwise_and(x, 15)
+        for grp in range(3):
             for ct in range(5):
-                q = (x + H1) * PS1 + RO1 + ct * 8
-                t0, e = G1f[pl.ds(q, 8)], G1f[pl.ds(q + RP1, 8)]
-                r = pl.ds(row(grp * 40 + ct * 8), 8)
-                Uf[r] = jnp.where(slot8 == j, pltpu.roll(jnp.where(l0, e, t0), jnp.bitwise_and(4 + 8 * j, 127), 1), Uf[r])
-                Df_[r] = jnp.where(slot8 == j, pltpu.roll(t0, 8 * j, 1), Df_[r])
-            return 0
-
-        lax.fori_loop(0, 33, pack1, 0)
+                up = dn = zero
+                for j in range(16 if grp < 2 else 1):
+                    q = (grp * 16 + j + H1) * PS1 + RO1 + ct * 8
+                    t0, e = G1f[q : q + 8], G1f[q + RP1 : q + RP1 + 8]
+                    up = jnp.where(slot8 == j, pltpu.roll(jnp.where(l0, e, t0), (4 + 8 * j) % 128, 1), up)
+                    dn = jnp.where(slot8 == j, pltpu.roll(t0, 8 * j, 1) if j else t0, dn)
+                b["U"][grp, ct * 8 : ct * 8 + 8] = up
+                b["D"][grp, ct * 8 : ct * 8 + 8] = dn
         G1 = b["G1"]
         msgs1 = []
 
@@ -391,43 +371,57 @@
             sy = XS1[dy][0]
             tiles = PAD8[XS1[dy][1]] // 8
             g0 = GS1[dx][0]
-
-            def unpack(k, _, dx=dx, dy=dy, sx=sx, sy=sy, tiles=tiles, g0=g0):
-                s = k + sx
-                grp, j = s // 16 - g0, jnp.bitwise_and(s, 15)
-                for ct in range(tiles):
-                    q = (k + (sx - N1 * dx + H1)) * PS1 + (sy - N1 * dy + RO1 + ct * 8)
-                    up = jnp.bitwise_and(124 - 8 * j, 127)
-                    u1 = pltpu.roll(b["RU1", dx, dy][grp, ct * 8 : ct * 8 + 8], up, 1)
-                    dn = pltpu.roll(b["RD", dx, dy][grp, ct * 8 : ct * 8 + 8], jnp.bitwise_and(128 - 8 * j, 127), 1)
-                    e = jnp.where(lane >= 124, u1, 0.0) + jnp.where(lane < 4, dn, 0.0)
-                    t0 = jnp.where(l0, u1, 0.0)
-                    if (dx, dy) != (0, 0):
-                        u0 = pltpu.roll(b["RU0", dx, dy][grp, ct * 8 : ct * 8 + 8], up, 1)
-                        e = e + jnp.where(l0, u0, 0.0)
-                        t0 = t0 + b["RT", dx, dy][k, ct * 8 : ct * 8 + 8]
-                    add1(q, t0)
-                    add1(q + RP1, e)
+            per = 11 if n == 33 else n
+
+            def unpack(i, _, dx=dx, dy=dy, sx=sx, sy=sy, tiles=tiles, g0=g0, per=per):
+                for p in range(per):
+                    k = i * per + p
+                    s = k + sx
+                    grp, j = s // 16 - g0, s % 16 if isinstance(s, int) else jnp.bitwise_and(s, 15)
+                    up = (124 - 8 * j) % 128 if isinstance(s, int) else jnp.bitwise_and(124 - 8 * j, 127)
+                    down = (128 - 8 * j) % 128 if isinstance(s, int) else jnp.bitwise_and(128 - 8 * j, 127)
+                    for ct in range(tiles):
+                        q = i * per * PS1 + ((p + (sx - N1 * dx + H1)) * PS1 + (sy - N1 * dy + RO1 + ct * 8))
+                        u1 = pltpu.roll(b["RU1", dx, dy][grp, ct * 8 : ct * 8 + 8], up, 1)
+                        dn = pltpu.roll(b["RD", dx, dy][grp, ct * 8 : ct * 8 + 8], down, 1)
+                        e = jnp.where(lane >= 124, u1, jnp.where(lane < 4, dn, 0.0))
+                        t0 = jnp.where(l0, u1, 0.0)
+                        if (dx, dy) != (0, 0):
+                            u0 = pltpu.roll(b["RU0", dx, dy][grp, ct * 8 : ct * 8 + 8], up, 1)
+                            e = e + jnp.where(l0, u0, 0.0)
+                            t0 = t0 + b["RT", dx, dy][k, ct * 8 : ct * 8 + 8]
+                        add1(q, t0)
+                        add1(q + RP1, e)
                 return 0
 
-            lax.fori_loop(0, n, unpack, 0)
+            if n == 33:
+                lax.fori_loop(0, 3, unpack, 0)
+            else:
+                unpack(0, 0)
 
         def ring1(Vf, op, emit, lo, hi):
-            def step(x, _):
-                for ct in range(5):
-                    q = row(x * PS1 + 8 + ct * 8)
-                    c = (Vf[pl.ds(q, 8)], Vf[pl.ds(q + RP1, 8)])
-                    for t in range(2):
-                        a, o = c[t], c[1 - t]
-                        zs = pltpu.roll(jnp.where(l127, o, a), 1, 1) + pltpu.roll(jnp.where(l0, o, a), 127, 1)
-                        s = q + t * RP1
-                        beside = (
-                            (Vf[pl.ds(s - PS1, 8)] + Vf[pl.ds(s + PS1, 8)]) + (Vf[pl.ds(s - 1, 8)] + Vf[pl.ds(s + 1, 8)]) + zs
-                        )
-                        emit(x, t, ct, s, op(a, beside, G1f[pl.ds(s, 8)]))
+            per = 3 if (hi - lo) % 3 == 0 else 2
+
+            def step(i, _):
+                for p in range(per):
+                    base = i * per * PS1
+                    for ct in range(5):
+                        q = row(base + ((p + lo + H1) * PS1 + 8 + ct * 8))
+                        c = (Vf[pl.ds(q, 8)], Vf[pl.ds(q + RP1, 8)])
+                        up = [pltpu.roll(v, 1, 1) for v in c]
+                        dn = [pltpu.roll(v, 127, 1) for v in c]
+                        for t in range(2):
+                            zs = jnp.where(l0, up[1 - t], up[t]) + jnp.where(l127, dn[1 - t], dn[t])
+                            s = q + t * RP1
+                            beside = (
+                                (Vf[pl.ds(s - PS1, 8)] + Vf[pl.ds(s + PS1, 8)])
+                                + (Vf[pl.ds(s - 1, 8)] + Vf[pl.ds(s + 1, 8)])
+                                + zs
+                            )
+                            emit(i * per * 40 + (p + lo + 1) * 40, t, ct, s, op(c[t], beside, G1f[pl.ds(s, 8)]))
                 return 0
 
-            lax.fori_loop(lo + H1, hi + H1, step, 0)
+            lax.fori_loop(0, (hi - lo) // per, step, 0)
 
         first = W / (6.0 * 0.25)
 
@@ -507,24 +501,25 @@
 
         lax.fori_loop(0, 4, spread, 0)
 
-        def coarse(Sf, Tf, lo, hi):
-            def step(k, _):
-                for ct in range(4):
-                    q = row(k * RP2 + 8 + ct * 8)
-                    a = Sf[pl.ds(q, 8)]
-                    beside = (
-                        (Sf[pl.ds(q - RP2, 8)] + Sf[pl.ds(q + RP2, 8)])
-                        + (Sf[pl.ds(q - 1, 8)] + Sf[pl.ds(q + 1, 8)])
-                        + (pltpu.roll(a, 1, 1) + pltpu.roll(a, 127, 1))
-                    )
-                    Tf[pl.ds(q, 8)] = (1.0 - W) * a + (C6 * beside + first2 * G2f[pl.ds(q, 8)])
+        def coarse(Sf, Tf, lo, n, per):
+            def step(i, _):
+                for p in range(per):
+                    for ct in range(4):
+                        q = row(i * per * RP2 + ((lo + p) * RP2 + 8 + ct * 8))
+                        a = Sf[pl.ds(q, 8)]
+                        beside = (
+                            (Sf[pl.ds(q - RP2, 8)] + Sf[pl.ds(q + RP2, 8)])
+                            + (Sf[pl.ds(q - 1, 8)] + Sf[pl.ds(q + 1, 8)])
+                            + (pltpu.roll(a, 1, 1) + pltpu.roll(a, 127, 1))
+                        )
+                        Tf[pl.ds(q, 8)] = (1.0 - W) * a + (C6 * beside + first2 * G2f[pl.ds(q, 8)])
                 return 0
 
-            lax.fori_loop(lo, hi, step, 0)
+            lax.fori_loop(0, n // per, step, 0)
 
         src, dst = VAf, VBf
-        for k in range(COARSE_SWEEPS - 1):
-            coarse(src, dst, 2 + k, 31 - k)
+        for lo, n, per in ((2, 28, 7), (2, 28, 7), (4, 24, 8), (4, 24, 8), (6, 20, 10)):
+            coarse(src, dst, lo, n, per)
             src, dst = dst, src
 
         f, c = grid(128, 256)
@@ -567,14 +562,14 @@
         def relax1(a, beside, g):
             return (1.0 - W) * a + (C6 * beside + first * g)
 
-        def put_l(x, t, ct, s, v):
-            L[pl.ds(row((x - (H1 - 1)) * 40 + ct * 8), 8), t * 128 : t * 128 + 128] = v
+        def put_l(r, t, ct, s, v):
+            L[pl.ds(row(r + ct * 8), 8), t * 128 : t * 128 + 128] = v
 
         ring1(WAf, relax1, put1(WBf), -2, 34)
         ring1(WBf, relax1, put_l, -1, 33)
 
         f, c = grid(256, 384)
-        gap = jnp.abs(jnp.where(c <= 256, c, jnp.where(c == 383, -1, 9999)) - 2 * jnp.where(f < 192, f, f - 256))
+        gap = jnp.abs(jnp.where(c < 256, c, jnp.where(c == 383, 256, jnp.where(c == 256, -1, 9999))) - 2 * jnp.where(f < 192, f, f - 256))
         P0 = jnp.where(gap == 0, 1.0, jnp.where(gap == 1, 0.5, 0.0)).astype(F32)
         CZ0f, F0f = flat(b["CZ0"]), flat(b["F0"])
 
@@ -611,23 +606,25 @@
                 add0(0, t, r, 0.5 * (get0(0, t, r) + get0(1, t, r)))
                 add0(65, t, r, get0(33, t, r))
 
-        def correct0(i, _):
-            for t in range(2):
-                for r in range(0, 80, 8):
-                    v, n = get0(i + 1, t, r), get0(i + 2, t, r)
-                    add0(2 * i + 1, t, r, v)
-                    add0(2 * i + 2, t, r, 0.5 * (v + n))
+        def correct0(k, _):
+            for i in (2 * k, 2 * k + 1):
+                for t in range(2):
+                    for r in range(0, 80, 8):
+                        v, n = get0(i + 1, t, r), get0(i + 2, t, r)
+                        add0(2 * i + 1, t, r, v)
+                        add0(2 * i + 2, t, r, 0.5 * (v + n))
             for yt in range(8):
-                v, n = get0(i + 1, 2, 8 + yt * 8), get0(i + 2, 2, 8 + yt * 8)
                 h = b["HR"][2, 0, yt * 8 : yt * 8 + 8]
-                for x, w in ((2 * i, v), (2 * i + 1, 0.5 * (v + n))):
-                    h = h + jnp.where(half == x, pltpu.roll(w, jnp.bitwise_and(2 * x, 127), 1), 0.0)
+                for i in (2 * k, 2 * k + 1):
+                    v, n = get0(i + 1, 2, 8 + yt * 8), get0(i + 2, 2, 8 + yt * 8)
+                    for x, w in ((2 * i, v), (2 * i + 1, 0.5 * (v + n))):
+                        h = h + jnp.where(half == x, pltpu.roll(w, jnp.bitwise_and(2 * x, 127), 1), 0.0)
                 b["HR"][2, 0, yt * 8 : yt * 8 + 8] = h
             return 0
 
-        lax.fori_loop(0, 32, correct0, 0)
-
-        stencil(Af, 2, relax0, storing(Bf, 3))
+        lax.fori_loop(0, 16, correct0, 0)
+
+        stencil(Af, Bf, 2, relax0, 3)
         msgs = faces(B, 3)
         tile = total_wait(2, sum_msgs)
         mean = jnp.sum(tile, keepdims=True) / cells
@@ -635,7 +632,7 @@
         for m in msgs:
             m.wait()
         merge(3)
-        stencil(Bf, 3, lambda c, beside, g: relax0(c, beside, g) - mean, storing(Af, None))
+        stencil(Bf, Af, 3, lambda c, beside, g: relax0(c, beside, g) - mean)
         outs = []
         for t in range(2):
             outs.append(pltpu.make_async_copy(A.at[1:65, t, 8:72, :], out_hbm.at[:, :, t * 128 : t * 128 + 128], local.at[4 + t]))

time: 142 us -> 90.6 us (0.64)
  Pallas kernels: 137 us -> 85.7 us
    pallas_call x1, Pallas kernels: 137 us -> 85.7 us  [shards(): pl.pallas_call(kernel, out_shape=jax.ShapeDtypeStruct(right_side.shape, F...]
where the time goes in v2:
time: 90.6 us; the launch traced here: 90.4 us
  Pallas kernels  85.7 us (95%)
  local copies, waits for them, and re-layouts  4.7 us (5%)
    pallas_call x1, Pallas kernels, shards(): pl.pallas_call(kernel, out_shape=jax.ShapeDtypeStruct(right_side.shape, F...  85.7 us
    unnamed x1, local copies, waits for them, and re-layouts  4.7 us

profile of v2, /device:TPU:0, one launch (start us, length us, event | category | flops | bytes accessed | tf_op | source)
XLA Modules:
  0.0 90.4 jit_solution(14141482466540894435)
XLA Ops:
  0.0 85.7 %shard_map.28 = f32[64,64,256]{2,1,0:T(8,128)} custom-call(f32[64,64,256]{2,1,0:T(8,128)} %g_hbm.1, f32[64,64,256]{2,1,0:T(8,128)} %v_hbm.1), custom_call_target="tpu_custom_call" | custom-call | tf_op jit(solution)/shard_map/pallas_call | solution.py:653
  85.7 4.7 %copy.4 = f32[64,64,256]{2,1,0:T(8,128)} copy(f32[64,64,256]{2,1,0:T(8,128)} %shard_map.28) | data formatting | bytes 8388608

commit v3 on v2

--- a/solution.py
+++ b/solution.py
@@ -39,12 +39,7 @@
 
 def make_kernel(nx, ny, nz):
     cells = float(nx * N0 * ny * N0 * nz * 256)
-    far = (
-        [(0, 0, k) for k in range(2, nz - 1)]
-        + [(0, k, 0) for k in range(2, ny - 1)]
-        + [(k, 0, 0) for k in range(2, nx - 1)]
-    )
-    peers = NEAR + far
+    peers = [d for d in NEAR if sum(map(abs, d)) == 1]
     ring = {0: [(0, 0, k) for k in range(1, nz)], 1: [(0, k, 0) for k in range(1, ny)], 2: [(k, 0, 0) for k in range(1, nx)]}
     n_sem = [0]
 
@@ -87,7 +82,7 @@
     N_MSG = 4 * 6 + 34 + 26 + (nx - 1) + (ny - 1) + (nz - 1)
     scratch += [pltpu.SemaphoreType.DMA((N_MSG,)), pltpu.SemaphoreType.DMA((N_MSG,)), pltpu.SemaphoreType.DMA((8,))]
 
-    def kernel(g_hbm, v_hbm, out_hbm, *refs):
+    def kernel(g_hbm, v_hbm, out_ref, *refs):
         b = dict(zip(names, refs))
         send, recv, local = refs[len(names):]
         A, B, G = b["A"], b["B"], b["G"]
@@ -163,7 +158,6 @@
             return 0
 
         lax.fori_loop(1, 65, clear_rows, 0)
-        pl.semaphore_wait(barrier, len(peers))
         loads[0].wait()
         loads[2].wait()
 
@@ -225,7 +219,11 @@
                             ys = Vf[pl.ds(q - 1, 8)] + Vf[pl.ds(q + 1, 8)]
                             beside = (c[p - 1, t] + c[p + 1, t]) + ys + zs[t]
                             g = Gf[pl.ds(row(x * 128 + t * 64 + yt * 8), 8)]
-                            Df[pl.ds(row(q), 8)] = op(c[p, t], beside, g)
+                            v = op(c[p, t], beside, g)
+                            if Df is None:
+                                out_ref[x, yt * 8 : yt * 8 + 8, t * 128 : t * 128 + 128] = v
+                            else:
+                                Df[pl.ds(row(q), 8)] = v
                             if summed:
                                 carry = (carry[0] + c[p, t], carry[1] + g)
                 return carry
@@ -259,6 +257,7 @@
             return 0
 
         lax.fori_loop(0, 8, pack_first, 0)
+        pl.semaphore_wait(barrier, len(peers))
         msgs = faces(A, 0)
         loads[1].wait()
         loads[3].wait()
@@ -632,14 +631,7 @@
         for m in msgs:
             m.wait()
         merge(3)
-        stencil(Bf, Af, 3, lambda c, beside, g: relax0(c, beside, g) - mean)
-        outs = []
-        for t in range(2):
-            outs.append(pltpu.make_async_copy(A.at[1:65, t, 8:72, :], out_hbm.at[:, :, t * 128 : t * 128 + 128], local.at[4 + t]))
-        for o in outs:
-            o.start()
-        for o in outs:
-            o.wait()
+        stencil(Bf, None, 3, lambda c, beside, g: relax0(c, beside, g) - mean)
 
     return kernel, scratch
 
@@ -652,11 +644,11 @@
         assert right_side.shape == (64, 64, 256)
         return pl.pallas_call(
             kernel,
-            out_shape=jax.ShapeDtypeStruct(right_side.shape, F32),
+            out_shape=pltpu.VMEM(right_side.shape, F32),
             in_specs=[pl.BlockSpec(memory_space=pl.ANY)] * 2,
-            out_specs=pl.BlockSpec(memory_space=pl.ANY),
+            out_specs=pl.BlockSpec(memory_space=pltpu.VMEM),
             scratch_shapes=scratch,
-            compiler_params=pltpu.CompilerParams(collective_id=0, has_side_effects=True, vmem_limit_bytes=60 << 20),
+            compiler_params=pltpu.CompilerParams(collective_id=0, has_side_effects=True, vmem_limit_bytes=54 << 20),
         )(right_side, initial_guess)
 
     placed = P("gx", "gy", "gz")

time: 90.6 us -> 84.3 us (0.930)
  Pallas kernels: 85.7 us -> 81.7 us
  local copies, waits for them, and re-layouts: 4.7 us -> 2.02 us
    pallas_call x1, Pallas kernels: 85.7 us -> 81.7 us  [shards(): pl.pallas_call(kernel, out_shape=pltpu.VMEM(right_side.shape, F32), in_sp...]
    unnamed x1, local copies, waits for them, and re-layouts: 4.7 us -> 2.02 us
where the time goes in v3:
time: 84.3 us; the launch traced here: 83.7 us
  Pallas kernels  81.7 us (97%)
  local copies, waits for them, and re-layouts  2.02 us (2%)
    pallas_call x1, Pallas kernels, shards(): pl.pallas_call(kernel, out_shape=pltpu.VMEM(right_side.shape, F32), in_sp...  81.7 us
    unnamed x1, local copies, waits for them, and re-layouts  2.02 us

profile of v3, /device:TPU:0, one launch (start us, length us, event | category | flops | bytes accessed | tf_op | source)
XLA Modules:
  0.0 83.7 jit_solution(12572726064996576185)
XLA Ops:
  0.0 81.7 %shard_map.28 = f32[64,64,256]{2,1,0:T(8,128)S(1)} custom-call(f32[64,64,256]{2,1,0:T(8,128)} %g_hbm.1, f32[64,64,256]{2,1,0:T(8,128)} %v_hbm.1), custom_call_target="tpu_custom_call" | custom-call | tf_op jit(solution)/shard_map/pallas_call | solution.py:645
  81.7 2.0 %copy.4 = f32[64,64,256]{2,1,0:T(8,128)} copy(f32[64,64,256]{2,1,0:T(8,128)S(1)} %shard_map.28) | data formatting | bytes 8388608

commit v4 on v3

--- a/solution.py
+++ b/solution.py
@@ -79,7 +79,7 @@
     for dx, dy in XY:
         vm(("RU1", dx, dy), GS1[dx][1], PAD8[XS1[dy][1]], 128)
         vm(("RD", dx, dy), GS1[dx][1], PAD8[XS1[dy][1]], 128)
-    N_MSG = 4 * 6 + 34 + 26 + (nx - 1) + (ny - 1) + (nz - 1)
+    N_MSG = 4 * 26 + 34 + 26 + (nx - 1) + (ny - 1) + (nz - 1)
     scratch += [pltpu.SemaphoreType.DMA((N_MSG,)), pltpu.SemaphoreType.DMA((N_MSG,)), pltpu.SemaphoreType.DMA((8,))]
 
     def kernel(g_hbm, v_hbm, out_ref, *refs):
@@ -91,7 +91,8 @@
         lane = lax.broadcasted_iota(jnp.int32, (8, 128), 1)
         l0, l127 = lane == 0, lane == 127
         zero = jnp.zeros((8, 128), F32)
-        used = [0]
+        used = [26 * 4]
+        refs_of = {}
 
         def at(d):
             return tuple(lax.rem(m + (k + n), n) if k else m for m, k, n in zip(me, d, sizes))
@@ -116,6 +117,7 @@
             return pl.multiple_of(k, m)
 
         Af, Bf, Gf = flat(A), flat(B), flat(G)
+        refs_of.update({id(Af): A, id(Bf): B})
         G1f, WAf, WBf = flat(b["G1"]), flat(b["WA"]), flat(b["WB"])
 
         def clear(ref):
@@ -163,75 +165,108 @@
 
         half = jnp.bitwise_and(lane + 1, 127) // 2
 
-        def faces(V, k):
-            pk = b["PK"].at[k]
-            return [
-                post(V.at[64, :, 8:72, :], V.at[0, :, 8:72, :], (1, 0, 0)),
-                post(V.at[1, :, 8:72, :], V.at[65, :, 8:72, :], (-1, 0, 0)),
-                post(V.at[1:65, :, 71:72, :], V.at[1:65, :, 7:8, :], (0, 1, 0)),
-                post(V.at[1:65, :, 8:9, :], V.at[1:65, :, 72:73, :], (0, -1, 0)),
-                post(pk, b["HR"].at[k, 0], (0, 0, 1)),
-                post(pk, b["HR"].at[k, 1], (0, 0, -1)),
-            ]
+        def pair(c):
+            return (c, 7 - c)
+
+        def chunk_msgs(V, k, c):
+            first_sem = 26 * k
+            out = []
+
+            def msg(j, src, dst, d):
+                out.append(
+                    pltpu.make_async_remote_copy(
+                        src_ref=src, dst_ref=dst, send_sem=send.at[j], recv_sem=recv.at[j], device_id=at(d), device_id_type=MESH
+                    )
+                )
+
+            for m, yt in enumerate(pair(c)):
+                r = pl.ds(row(8 + yt * 8), 8)
+                msg(first_sem + c * 6 + m, V.at[64, :, r, :], V.at[0, :, r, :], (1, 0, 0))
+                msg(first_sem + c * 6 + 2 + m, V.at[1, :, r, :], V.at[65, :, r, :], (-1, 0, 0))
+            r = pl.ds(row(c * 16, 16), 16)
+            pk = b["PK"].at[k, r, :]
+            msg(first_sem + c * 6 + 4, pk, b["HR"].at[k, 0, r, :], (0, 0, 1))
+            msg(first_sem + c * 6 + 5, pk, b["HR"].at[k, 1, r, :], (0, 0, -1))
+            if isinstance(c, int) and c == 0:
+                msg(first_sem + 24, V.at[1:65, :, 71:72, :], V.at[1:65, :, 7:8, :], (0, 1, 0))
+                msg(first_sem + 25, V.at[1:65, :, 8:9, :], V.at[1:65, :, 72:73, :], (0, -1, 0))
+            return out
 
         odd = jnp.bitwise_and(lane, 1) == 1
 
-        def merge(k):
-            for yt in range(8):
-                r = slice(yt * 8, yt * 8 + 8)
+        def take_chunk(V, k, c):
+            for m in chunk_msgs(V, k, c):
+                m.wait()
+            for m in range(2):
+                r = pl.ds(row(c * 16 + 8 * m), 8)
                 b["HR"][k, 0, r] = jnp.where(odd, pltpu.roll(b["HR"][k, 1, r], 127, 1), pltpu.roll(b["HR"][k, 0, r], 1, 1))
 
-        def put_faces(Df, k, i):
-            for yt in range(8):
-                keep = b["PK"][k, yt * 8 : yt * 8 + 8]
-                for p in range(4):
-                    x = i * 4 + p
-                    r = row((i * 4 + 1) * PS0) + (p * PS0 + 8 + yt * 8)
-                    both = jnp.where(l0, Df[pl.ds(r, 8)], Df[pl.ds(r + RP0, 8)])
-                    both = pltpu.roll(both, jnp.bitwise_and(2 * x, 127), 1)
-                    keep = jnp.where(half == x, both, keep)
-                b["PK"][k, yt * 8 : yt * 8 + 8] = keep
-
-        def stencil(Vf, Df, k, op, faces_to=None, carry=0):
+        def put_faces(Df, k, blocks, c):
+            for m, yt in enumerate(pair(c)):
+                r = pl.ds(row(c * 16 + 8 * m), 8)
+                keep = b["PK"][k, r]
+                for i in blocks:
+                    for p in range(16):
+                        x = i * 16 + p
+                        q = row((i * 16 + 1) * PS0 + 8 + yt * 8) + p * PS0
+                        both = jnp.where(l0, Df[pl.ds(row(q), 8)], Df[pl.ds(row(q + RP0), 8)])
+                        both = pltpu.roll(both, jnp.bitwise_and(2 * x, 127), 1)
+                        keep = jnp.where(half == x, both, keep)
+                b["PK"][k, r] = keep
+
+        def stencil(Vf, Df, k, op, faces_to=None, carry=0, taken=False):
             summed = isinstance(carry, tuple)
-
-            def step(i, carry):
-                base = row((i * 4 + 1) * PS0)
+            V, Dst = refs_of[id(Vf)], refs_of.get(id(Df))
+
+            def chunk(c, carry):
+                if not taken:
+                    take_chunk(V, k, c)
+
+                def step(i, carry):
+                    base = row((i * 16 + 1) * PS0)
+                    if faces_to is not None:
+                        put_faces(Df, faces_to, (jnp.maximum(i - 1, 0),), c)
+                    for m, yt in enumerate(pair(c)):
+                        o = 8 + yt * 8
+                        h = b["HR"][k, 0, pl.ds(row(c * 16 + 8 * m), 8)]
+
+                        def get(p, t):
+                            return Vf[pl.ds(row(base + o + (p * PS0 + t * RP0)), 8)]
+
+                        below, mid = [get(-1, t) for t in range(2)], [get(0, t) for t in range(2)]
+                        for p in range(16):
+                            x = i * 16 + p
+                            above = [get(p + 1, t) for t in range(2)]
+                            e = pltpu.roll(h, jnp.bitwise_and(128 - 2 * x, 127), 1)
+                            c0, c1 = mid
+                            up0, up1, dn0, dn1 = (pltpu.roll(v, n, 1) for n in (1, 127) for v in (c0, c1))
+                            zs = (
+                                jnp.where(l0, e, up0) + jnp.where(l127, dn1, dn0),
+                                jnp.where(l0, up0, up1) + jnp.where(l127, e, dn1),
+                            )
+                            for t in range(2):
+                                q = base + o + (p * PS0 + t * RP0)
+                                ys = Vf[pl.ds(q - 1, 8)] + Vf[pl.ds(q + 1, 8)]
+                                beside = (below[t] + above[t]) + ys + zs[t]
+                                g = Gf[pl.ds(row(x * 128 + t * 64 + yt * 8), 8)]
+                                v = op(mid[t], beside, g)
+                                if Df is None:
+                                    out_ref[x, pl.ds(row(yt * 8), 8), t * 128 : t * 128 + 128] = v
+                                else:
+                                    Df[pl.ds(row(q), 8)] = v
+                                if summed:
+                                    carry = (carry[0] + mid[t], carry[1] + g)
+                            below, mid = mid, above
+                    return carry
+
+                carry = lax.fori_loop(0, 4, step, carry)
                 if faces_to is not None:
-                    put_faces(Df, faces_to, jnp.maximum(i - 1, 0))
-                for yt in range(8):
-                    o = 8 + yt * 8
-                    c = {
-                        (p, t): Vf[pl.ds(row(base + (p * PS0 + t * RP0 + o)), 8)] for p in range(-1, 5) for t in range(2)
-                    }
-                    h = b["HR"][k, 0, yt * 8 : yt * 8 + 8]
-                    for p in range(4):
-                        x = i * 4 + p
-                        e = pltpu.roll(h, jnp.bitwise_and(128 - 2 * x, 127), 1)
-                        c0, c1 = c[p, 0], c[p, 1]
-                        up0, up1, dn0, dn1 = (pltpu.roll(v, n, 1) for n in (1, 127) for v in (c0, c1))
-                        zs = (
-                            jnp.where(l0, e, up0) + jnp.where(l127, dn1, dn0),
-                            jnp.where(l0, up0, up1) + jnp.where(l127, e, dn1),
-                        )
-                        for t in range(2):
-                            q = base + (p * PS0 + t * RP0 + o)
-                            ys = Vf[pl.ds(q - 1, 8)] + Vf[pl.ds(q + 1, 8)]
-                            beside = (c[p - 1, t] + c[p + 1, t]) + ys + zs[t]
-                            g = Gf[pl.ds(row(x * 128 + t * 64 + yt * 8), 8)]
-                            v = op(c[p, t], beside, g)
-                            if Df is None:
-                                out_ref[x, yt * 8 : yt * 8 + 8, t * 128 : t * 128 + 128] = v
-                            else:
-                                Df[pl.ds(row(q), 8)] = v
-                            if summed:
-                                carry = (carry[0] + c[p, t], carry[1] + g)
+                    put_faces(Df, faces_to, (3,), c)
+                    for m in chunk_msgs(Dst, faces_to, c):
+                        m.start()
                 return carry
 
-            carry = lax.fori_loop(0, 16, step, carry)
-            if faces_to is not None:
-                put_faces(Df, faces_to, 15)
-            return carry
+            return lax.fori_loop(1, 4, chunk, chunk(0, carry))
 
         def relax0(c, beside, g):
             return (1.0 - W) * c + C6 * (beside + g)
@@ -251,31 +286,22 @@
                 tile = tile + b[f"TR{stage}"][j]
             return tile
 
-        def pack_first(i, _):
-            put_faces(Af, 0, 2 * i)
-            put_faces(Af, 0, 2 * i + 1)
+        def pack_first(n, _):
+            i = jnp.bitwise_and(n, 1) * 2
+            put_faces(Af, 0, (i, i + 1), n // 2)
             return 0
 
         lax.fori_loop(0, 8, pack_first, 0)
         pl.semaphore_wait(barrier, len(peers))
-        msgs = faces(A, 0)
+        for c in range(4):
+            for m in chunk_msgs(A, 0, c):
+                m.start()
         loads[1].wait()
         loads[3].wait()
-        for m in msgs:
-            m.wait()
-        merge(0)
         sums = stencil(Af, Bf, 0, relax0, 1, (zero, zero))
-        msgs = faces(B, 1)
         sum_msgs = total_stage(0, sums[0] + shift_weight() * sums[1])
-        for m in msgs:
-            m.wait()
-        merge(1)
         stencil(Bf, Af, 1, relax0, 2)
-        msgs = faces(A, 2)
         sum_msgs = total_stage(1, total_wait(0, sum_msgs))
-        for m in msgs:
-            m.wait()
-        merge(2)
 
         stencil(Af, Bf, 2, defect0)
 
@@ -613,24 +639,21 @@
                         add0(2 * i + 1, t, r, v)
                         add0(2 * i + 2, t, r, 0.5 * (v + n))
             for yt in range(8):
-                h = b["HR"][2, 0, yt * 8 : yt * 8 + 8]
+                place = 16 * yt if yt < 4 else 16 * (7 - yt) + 8
+                h = b["HR"][2, 0, place : place + 8]
                 for i in (2 * k, 2 * k + 1):
                     v, n = get0(i + 1, 2, 8 + yt * 8), get0(i + 2, 2, 8 + yt * 8)
                     for x, w in ((2 * i, v), (2 * i + 1, 0.5 * (v + n))):
                         h = h + jnp.where(half == x, pltpu.roll(w, jnp.bitwise_and(2 * x, 127), 1), 0.0)
-                b["HR"][2, 0, yt * 8 : yt * 8 + 8] = h
+                b["HR"][2, 0, place : place + 8] = h
             return 0
 
         lax.fori_loop(0, 16, correct0, 0)
 
-        stencil(Af, Bf, 2, relax0, 3)
-        msgs = faces(B, 3)
+        stencil(Af, Bf, 2, relax0, 3, taken=True)
         tile = total_wait(2, sum_msgs)
         mean = jnp.sum(tile, keepdims=True) / cells
         mean = jnp.broadcast_to(mean, (8, 128))
-        for m in msgs:
-            m.wait()
-        merge(3)
         stencil(Bf, None, 3, lambda c, beside, g: relax0(c, beside, g) - mean)
 
     return kernel, scratch

time: 84.3 us -> 77.4 us (0.918)
  Pallas kernels: 81.7 us -> 75.2 us
    pallas_call x1, Pallas kernels: 81.7 us -> 75.2 us  [shards(): pl.pallas_call(kernel, out_shape=pltpu.VMEM(right_side.shape, F32), in_sp...]
where the time goes in v4:
time: 77.4 us; the launch traced here: 77.3 us
  Pallas kernels  75.2 us (97%)
  local copies, waits for them, and re-layouts  2.02 us (3%)
    pallas_call x1, Pallas kernels, shards(): pl.pallas_call(kernel, out_shape=pltpu.VMEM(right_side.shape, F32), in_sp...  75.2 us
    unnamed x1, local copies, waits for them, and re-layouts  2.02 us

profile of v4, /device:TPU:0, one launch (start us, length us, event | category | flops | bytes accessed | tf_op | source)
XLA Modules:
  0.0 77.3 jit_solution(9630873818175074473)
XLA Ops:
  0.0 75.2 %shard_map.28 = f32[64,64,256]{2,1,0:T(8,128)S(1)} custom-call(f32[64,64,256]{2,1,0:T(8,128)} %g_hbm.1, f32[64,64,256]{2,1,0:T(8,128)} %v_hbm.1), custom_call_target="tpu_custom_call" | custom-call | tf_op jit(solution)/shard_map/pallas_call | solution.py:668
  75.2 2.0 %copy.4 = f32[64,64,256]{2,1,0:T(8,128)} copy(f32[64,64,256]{2,1,0:T(8,128)S(1)} %shard_map.28) | data formatting | bytes 8388608

commit v5 on v4

--- a/solution.py
+++ b/solution.py
@@ -12,7 +12,7 @@
 COARSE_SWEEPS = 6
 W = 0.8
 C6 = W / 6.0
-HIGH = lax.Precision.HIGHEST
+BF16 = jnp.bfloat16
 
 N0, RP0 = 64, 96
 PS0 = 2 * RP0
@@ -50,14 +50,15 @@
         scratch.append(pltpu.VMEM(shape, F32))
 
     vm("A", 66, 2, RP0, 128)
-    vm("B", 67, 2, RP0, 128)
+    vm("B", 66, 2, RP0, 128)
+    vm("C", 67, 2, RP0, 128)
     vm("G", 64, 2, 64, 128)
     vm("PK", 4, 64, 128)
     vm("HR", 4, 2, 64, 128)
     vm("L", 1360, 256)
-    vm("G1", 41, 2, RP1, 128)
-    vm("WA", 41, 2, RP1, 128)
-    vm("WB", 41, 2, RP1, 128)
+    vm("G1", 42, 2, RP1, 128)
+    vm("WA", 42, 2, RP1, 128)
+    vm("WB", 42, 2, RP1, 128)
     vm("U", 3, 40, 128)
     vm("D", 3, 40, 128)
     vm("G2", 32, RP2, 128)
@@ -85,7 +86,7 @@
     def kernel(g_hbm, v_hbm, out_ref, *refs):
         b = dict(zip(names, refs))
         send, recv, local = refs[len(names):]
-        A, B, G = b["A"], b["B"], b["G"]
+        A, B, C, G = b["A"], b["B"], b["C"], b["G"]
         me = (lax.axis_index("gx"), lax.axis_index("gy"), lax.axis_index("gz"))
         sizes = (nx, ny, nz)
         lane = lax.broadcasted_iota(jnp.int32, (8, 128), 1)
@@ -116,7 +117,7 @@
         def row(k, m=8):
             return pl.multiple_of(k, m)
 
-        Af, Bf, Gf = flat(A), flat(B), flat(G)
+        Af, Bf, Cf, Gf = flat(A), flat(B), flat(C), flat(G)
         refs_of.update({id(Af): A, id(Bf): B})
         G1f, WAf, WBf = flat(b["G1"]), flat(b["WA"]), flat(b["WB"])
 
@@ -149,14 +150,13 @@
             if isinstance(name, tuple):
                 clear(b[name])
         clear(b["G1"])
-        for dst in (B.at[0], B.at[65], B.at[66]):
+        for dst in (C.at[0], C.at[65], C.at[66]):
             clear(dst)
 
         def clear_rows(i, _):
             for t in range(2):
-                Bf[pl.ds(row(i * PS0 + t * RP0), 8)] = zero
-                for r in (72, 80, 88):
-                    Bf[pl.ds(row(i * PS0 + t * RP0 + r), 8)] = zero
+                for r in (0, 72, 80, 88):
+                    Cf[pl.ds(row(i * PS0 + t * RP0 + r), 8)] = zero
             return 0
 
         lax.fori_loop(1, 65, clear_rows, 0)
@@ -303,17 +303,8 @@
         stencil(Bf, Af, 1, relax0, 2)
         sum_msgs = total_stage(1, total_wait(0, sum_msgs))
 
-        stencil(Af, Bf, 2, defect0)
-
-        def clear_rims(i, _):
-            for t in range(2):
-                Bf[pl.ds(i * PS0 + t * RP0 + 7, 1)] = zero[0:1]
-                Bf[pl.ds(i * PS0 + t * RP0 + 72, 1)] = zero[0:1]
-            return 0
-
-        lax.fori_loop(1, 65, clear_rims, 0)
-        for dst in (B.at[0], B.at[65]):
-            clear(dst)
+        stencil(Af, Cf, 2, defect0)
+
         L = b["L"]
 
         def restrict_xy(Df, plane, slab, start):
@@ -328,11 +319,18 @@
             for t in range(2):
                 for ct in range(5):
                     L[pl.ds(row(i * 40 + ct * 8), 8), t * 128 : t * 128 + 128] = restrict_xy(
-                        Bf, i * 2 * PS0, PS0, t * RP0 + 7 + 16 * ct
+                        Cf, i * 2 * PS0, PS0, t * RP0 + 7 + 16 * ct
                     )
             return 0
 
         lax.fori_loop(0, 33, restrict0, 0)
+
+        def exact_dot(x, weights):
+            hi = x.astype(BF16)
+            rest = x - hi.astype(F32)
+            mid = rest.astype(BF16)
+            lo = (rest - mid.astype(F32)).astype(BF16)
+            return sum(jnp.dot(part, weights, preferred_element_type=F32) for part in (lo, mid, hi))
 
         def grid(rows, cols):
             return (
@@ -342,10 +340,10 @@
 
         f, c = grid(256, 256)
         gap = jnp.abs(f - 2 * c)
-        R0 = jnp.where(gap == 0, 0.5, jnp.where(gap == 1, 0.25, 0.0)).astype(F32)
+        R0 = jnp.where(gap == 0, 0.5, jnp.where(gap == 1, 0.25, 0.0)).astype(BF16)
 
         def rz0(i, _):
-            res = jnp.dot(L[pl.ds(row(i * 440), 440), :], R0, precision=HIGH, preferred_element_type=F32)
+            res = exact_dot(L[pl.ds(row(i * 440), 440), :], R0)
             for p in range(11):
                 for t in range(2):
                     for ct in range(5):
@@ -373,7 +371,13 @@
         def along(spec, k, off=0):
             return slice(spec[k][0] + off, spec[k][0] + off + spec[k][1])
 
-        for dx, dy in XY:
+        for dx, dy in sorted(XY, key=lambda d: -abs(d[0]) - abs(d[1])):
+            n = XS1[dy][1]
+            ys = along(XS1, dy)
+            gs = along(GS1, dx)
+            msgs1.append(post(b["U"].at[gs, ys, :], b["RU1", dx, dy].at[:, 0:n, :], (dx, dy, 1)))
+            msgs1.append(post(b["D"].at[gs, ys, :], b["RD", dx, dy].at[:, 0:n, :], (dx, dy, -1)))
+        for dx, dy in sorted(XY, key=lambda d: -abs(d[0]) - abs(d[1])):
             n = XS1[dy][1]
             ys = along(XS1, dy)
             gs = along(GS1, dx)
@@ -382,8 +386,6 @@
                     post(G1.at[along(XS1, dx, H1), 0, along(XS1, dy, RO1), :], b["RT", dx, dy].at[:, 0:n, :], (dx, dy, 0))
                 )
                 msgs1.append(post(b["U"].at[gs, ys, :], b["RU0", dx, dy].at[:, 0:n, :], (dx, dy, 0)))
-            msgs1.append(post(b["U"].at[gs, ys, :], b["RU1", dx, dy].at[:, 0:n, :], (dx, dy, 1)))
-            msgs1.append(post(b["D"].at[gs, ys, :], b["RD", dx, dy].at[:, 0:n, :], (dx, dy, -1)))
         sum_msgs = total_stage(2, total_wait(1, sum_msgs))
         for m in msgs1:
             m.wait()
@@ -424,8 +426,7 @@
             else:
                 unpack(0, 0)
 
-        def ring1(Vf, op, emit, lo, hi):
-            per = 3 if (hi - lo) % 3 == 0 else 2
+        def ring1(Vf, op, emit, lo, hi, per):
 
             def step(i, _):
                 for p in range(per):
@@ -456,8 +457,8 @@
 
             return emit
 
-        ring1(G1f, lambda a, beside, g: ((2.0 - W) * first) * a + (C6 * first) * beside, put1(WAf), -3, 35)
-        ring1(WAf, lambda a, beside, g: g - 0.25 * (6.0 * a - beside), put1(WBf), -1, 32)
+        ring1(G1f, lambda a, beside, g: ((2.0 - W) * first) * a + (C6 * first) * beside, put1(WAf), -3, 37, 10)
+        ring1(WAf, lambda a, beside, g: g - 0.25 * (6.0 * a - beside), put1(WBf), -1, 32, 11)
 
         def restrict1(i, _):
             for t in range(2):
@@ -470,10 +471,10 @@
         lax.fori_loop(0, 16, restrict1, 0)
         f, c = grid(256, 128)
         gap = jnp.abs(jnp.where(f < 192, f, f - 256) - 2 * c)
-        R1 = jnp.where(c < 64, jnp.where(gap == 0, 0.5, jnp.where(gap == 1, 0.25, 0.0)), 0.0).astype(F32)
+        R1 = jnp.where(c < 64, jnp.where(gap == 0, 0.5, jnp.where(gap == 1, 0.25, 0.0)), 0.0).astype(BF16)
         G2, VA, VB = b["G2"], b["VA"], b["VB"]
         G2f, VAf, VBf = flat(G2), flat(VA), flat(VB)
-        res = jnp.dot(L[0:256, :], R1, precision=HIGH, preferred_element_type=F32)
+        res = exact_dot(L[0:256, :], R1)
         slot16 = lane // 16
         for x in range(16):
             for ct in range(2):
@@ -487,21 +488,21 @@
                     acc = jnp.where(slot16 == j, pltpu.roll(v, 16 * j, 1) if j else v, acc)
                 b["PZ2"][grp, ct * 8 : ct * 8 + 8] = acc
         msgs2 = []
-        for dx, dy in XY:
-            px, py = along(XS2, dx), along(XS2, dy)
-            if (dx, dy) != (0, 0):
-                msgs2.append(
-                    post(
-                        G2.at[along(XS2, dx, H2), along(XS2, dy, RO2), :],
-                        G2.at[along(XS2, dx, H2 - N2 * dx), along(XS2, dy, RO2 - N2 * dy), :],
-                        (dx, dy, 0),
-                    )
-                )
+        for dx, dy in sorted(XY, key=lambda d: -abs(d[0]) - abs(d[1])):
+            py = along(XS2, dy)
             gs = along(GS2, dx)
             gd = along(GS2, dx, 1 - 2 * dx)
             yd = along(XS2, dy, 8 - N2 * dy)
             for side, dz in ((0, 1), (1, -1)):
                 msgs2.append(post(b["PZ2"].at[gs, py, :], b["RZ2"].at[side, gd, yd, :], (dx, dy, dz)))
+        for dx, dy in sorted(XY8, key=lambda d: -abs(d[0]) - abs(d[1])):
+            msgs2.append(
+                post(
+                    G2.at[along(XS2, dx, H2), along(XS2, dy, RO2), :],
+                    G2.at[along(XS2, dx, H2 - N2 * dx), along(XS2, dy, RO2 - N2 * dy), :],
+                    (dx, dy, 0),
+                )
+            )
         for m in msgs2:
             m.wait()
 
@@ -549,11 +550,11 @@
 
         f, c = grid(128, 256)
         gap = jnp.abs(jnp.where(c < 192, c, c - 256) - 2 * jnp.where(f < 96, f, f - 128))
-        P1 = jnp.where(gap == 0, 1.0, jnp.where(gap == 1, 0.5, 0.0)).astype(F32)
+        P1 = jnp.where(gap == 0, 1.0, jnp.where(gap == 1, 0.5, 0.0)).astype(BF16)
         CZ1f, F1f = flat(b["CZ1"]), flat(b["F1"])
         for k in range(20):
             L[k * 24 : k * 24 + 24, 0:128] = src[pl.ds((k + 6) * RP2 + 12, 24)]
-        res = jnp.dot(L[0:480, 0:128], P1, precision=HIGH, preferred_element_type=F32)
+        res = exact_dot(L[0:480, 0:128], P1)
         for k in range(20):
             for t in range(2):
                 b["CZ1"][k, t, 0:24] = res[k * 24 : k * 24 + 24, t * 128 : t * 128 + 128]
@@ -590,16 +591,16 @@
         def put_l(r, t, ct, s, v):
             L[pl.ds(row(r + ct * 8), 8), t * 128 : t * 128 + 128] = v
 
-        ring1(WAf, relax1, put1(WBf), -2, 34)
-        ring1(WBf, relax1, put_l, -1, 33)
+        ring1(WAf, relax1, put1(WBf), -2, 34, 9)
+        ring1(WBf, relax1, put_l, -1, 33, 17)
 
         f, c = grid(256, 384)
         gap = jnp.abs(jnp.where(c < 256, c, jnp.where(c == 383, 256, jnp.where(c == 256, -1, 9999))) - 2 * jnp.where(f < 192, f, f - 256))
-        P0 = jnp.where(gap == 0, 1.0, jnp.where(gap == 1, 0.5, 0.0)).astype(F32)
+        P0 = jnp.where(gap == 0, 1.0, jnp.where(gap == 1, 0.5, 0.0)).astype(BF16)
         CZ0f, F0f = flat(b["CZ0"]), flat(b["F0"])
 
         def pz0(i, _):
-            res = jnp.dot(L[pl.ds(row(i * 680), 680), :], P0, precision=HIGH, preferred_element_type=F32)
+            res = exact_dot(L[pl.ds(row(i * 680), 680), :], P0)
             for p in range(17):
                 for t in range(3):
                     CZ0f[pl.ds(row((i * 17 + p) * 144 + t * 48), 40)] = res[p * 40 : p * 40 + 40, t * 128 : t * 128 + 128]

time: 77.4 us -> 70.2 us (0.907)
  Pallas kernels: 75.2 us -> 67.3 us
    pallas_call x1, Pallas kernels: 75.2 us -> 67.3 us  [shards(): pl.pallas_call(kernel, out_shape=pltpu.VMEM(right_side.shape, F32), in_sp...]
where the time goes in v5:
time: 70.2 us; the launch traced here: 69.3 us
  Pallas kernels  67.3 us (96%)
  local copies, waits for them, and re-layouts  2.02 us (3%)
    pallas_call x1, Pallas kernels, shards(): pl.pallas_call(kernel, out_shape=pltpu.VMEM(right_side.shape, F32), in_sp...  67.3 us
    unnamed x1, local copies, waits for them, and re-layouts  2.02 us

profile of v5, /device:TPU:0, one launch (start us, length us, event | category | flops | bytes accessed | tf_op | source)
XLA Modules:
  0.0 69.3 jit_solution(613092124275717275)
XLA Ops:
  0.0 67.3 %shard_map.28 = f32[64,64,256]{2,1,0:T(8,128)S(1)} custom-call(f32[64,64,256]{2,1,0:T(8,128)} %g_hbm.1, f32[64,64,256]{2,1,0:T(8,128)} %v_hbm.1), custom_call_target="tpu_custom_call" | custom-call | tf_op jit(solution)/shard_map/pallas_call | solution.py:669
  67.3 2.0 %copy.4 = f32[64,64,256]{2,1,0:T(8,128)} copy(f32[64,64,256]{2,1,0:T(8,128)S(1)} %shard_map.28) | data formatting | bytes 8388608

commit v6 on v5

--- a/solution.py
+++ b/solution.py
@@ -80,7 +80,7 @@
     for dx, dy in XY:
         vm(("RU1", dx, dy), GS1[dx][1], PAD8[XS1[dy][1]], 128)
         vm(("RD", dx, dy), GS1[dx][1], PAD8[XS1[dy][1]], 128)
-    N_MSG = 4 * 26 + 34 + 26 + (nx - 1) + (ny - 1) + (nz - 1)
+    N_MSG = 4 * 28 + 34 + 26 + (nx - 1) + (ny - 1) + (nz - 1)
     scratch += [pltpu.SemaphoreType.DMA((N_MSG,)), pltpu.SemaphoreType.DMA((N_MSG,)), pltpu.SemaphoreType.DMA((8,))]
 
     def kernel(g_hbm, v_hbm, out_ref, *refs):
@@ -92,7 +92,7 @@
         lane = lax.broadcasted_iota(jnp.int32, (8, 128), 1)
         l0, l127 = lane == 0, lane == 127
         zero = jnp.zeros((8, 128), F32)
-        used = [26 * 4]
+        used = [28 * 4]
         refs_of = {}
 
         def at(d):
@@ -168,16 +168,24 @@
         def pair(c):
             return (c, 7 - c)
 
+        def message(j, src, dst, d):
+            return pltpu.make_async_remote_copy(
+                src_ref=src, dst_ref=dst, send_sem=send.at[j], recv_sem=recv.at[j], device_id=at(d), device_id_type=MESH
+            )
+
+        def row_msgs(V, k, h):
+            ps = slice(1 + 32 * h, 33 + 32 * h)
+            return [
+                message(28 * k + 24 + 2 * h, V.at[ps, :, 71:72, :], V.at[ps, :, 7:8, :], (0, 1, 0)),
+                message(28 * k + 25 + 2 * h, V.at[ps, :, 8:9, :], V.at[ps, :, 72:73, :], (0, -1, 0)),
+            ]
+
         def chunk_msgs(V, k, c):
-            first_sem = 26 * k
+            first_sem = 28 * k
             out = []
 
             def msg(j, src, dst, d):
-                out.append(
-                    pltpu.make_async_remote_copy(
-                        src_ref=src, dst_ref=dst, send_sem=send.at[j], recv_sem=recv.at[j], device_id=at(d), device_id_type=MESH
-                    )
-                )
+                out.append(message(j, src, dst, d))
 
             for m, yt in enumerate(pair(c)):
                 r = pl.ds(row(8 + yt * 8), 8)
@@ -187,9 +195,6 @@
             pk = b["PK"].at[k, r, :]
             msg(first_sem + c * 6 + 4, pk, b["HR"].at[k, 0, r, :], (0, 0, 1))
             msg(first_sem + c * 6 + 5, pk, b["HR"].at[k, 1, r, :], (0, 0, -1))
-            if isinstance(c, int) and c == 0:
-                msg(first_sem + 24, V.at[1:65, :, 71:72, :], V.at[1:65, :, 7:8, :], (0, 1, 0))
-                msg(first_sem + 25, V.at[1:65, :, 8:9, :], V.at[1:65, :, 72:73, :], (0, -1, 0))
             return out
 
         odd = jnp.bitwise_and(lane, 1) == 1
@@ -259,7 +264,17 @@
                             below, mid = mid, above
                     return carry
 
-                carry = lax.fori_loop(0, 4, step, carry)
+                if isinstance(c, int):
+                    for h in range(2):
+                        if not taken:
+                            for m in row_msgs(V, k, h):
+                                m.wait()
+                        carry = lax.fori_loop(2 * h, 2 * h + 2, step, carry)
+                        if faces_to is not None:
+                            for m in row_msgs(Dst, faces_to, h):
+                                m.start()
+                else:
+                    carry = lax.fori_loop(0, 4, step, carry)
                 if faces_to is not None:
                     put_faces(Df, faces_to, (3,), c)
                     for m in chunk_msgs(Dst, faces_to, c):
@@ -296,6 +311,9 @@
         for c in range(4):
             for m in chunk_msgs(A, 0, c):
                 m.start()
+            if c == 0:
+                for m in row_msgs(A, 0, 0) + row_msgs(A, 0, 1):
+                    m.start()
         loads[1].wait()
         loads[3].wait()
         sums = stencil(Af, Bf, 0, relax0, 1, (zero, zero))
@@ -371,21 +389,25 @@
         def along(spec, k, off=0):
             return slice(spec[k][0] + off, spec[k][0] + off + spec[k][1])
 
-        for dx, dy in sorted(XY, key=lambda d: -abs(d[0]) - abs(d[1])):
+        def packed1(dx, dy):
             n = XS1[dy][1]
-            ys = along(XS1, dy)
-            gs = along(GS1, dx)
+            ys, gs = along(XS1, dy), along(GS1, dx)
             msgs1.append(post(b["U"].at[gs, ys, :], b["RU1", dx, dy].at[:, 0:n, :], (dx, dy, 1)))
             msgs1.append(post(b["D"].at[gs, ys, :], b["RD", dx, dy].at[:, 0:n, :], (dx, dy, -1)))
-        for dx, dy in sorted(XY, key=lambda d: -abs(d[0]) - abs(d[1])):
+
+        corners = [d for d in XY if d[0] and d[1]]
+        for dx, dy in corners:
+            packed1(dx, dy)
+        for dx, dy in [d for d in XY8 if d not in corners] + corners:
             n = XS1[dy][1]
-            ys = along(XS1, dy)
-            gs = along(GS1, dx)
-            if (dx, dy) != (0, 0):
-                msgs1.append(
-                    post(G1.at[along(XS1, dx, H1), 0, along(XS1, dy, RO1), :], b["RT", dx, dy].at[:, 0:n, :], (dx, dy, 0))
-                )
-                msgs1.append(post(b["U"].at[gs, ys, :], b["RU0", dx, dy].at[:, 0:n, :], (dx, dy, 0)))
+            msgs1.append(
+                post(G1.at[along(XS1, dx, H1), 0, along(XS1, dy, RO1), :], b["RT", dx, dy].at[:, 0:n, :], (dx, dy, 0))
+            )
+        for dx, dy in [d for d in XY if d not in corners]:
+            packed1(dx, dy)
+        for dx, dy in XY8:
+            n = XS1[dy][1]
+            msgs1.append(post(b["U"].at[along(GS1, dx), along(XS1, dy), :], b["RU0", dx, dy].at[:, 0:n, :], (dx, dy, 0)))
         sum_msgs = total_stage(2, total_wait(1, sum_msgs))
         for m in msgs1:
             m.wait()
@@ -488,14 +510,17 @@
                     acc = jnp.where(slot16 == j, pltpu.roll(v, 16 * j, 1) if j else v, acc)
                 b["PZ2"][grp, ct * 8 : ct * 8 + 8] = acc
         msgs2 = []
-        for dx, dy in sorted(XY, key=lambda d: -abs(d[0]) - abs(d[1])):
-            py = along(XS2, dy)
+        def packed2(dx, dy):
             gs = along(GS2, dx)
             gd = along(GS2, dx, 1 - 2 * dx)
             yd = along(XS2, dy, 8 - N2 * dy)
             for side, dz in ((0, 1), (1, -1)):
-                msgs2.append(post(b["PZ2"].at[gs, py, :], b["RZ2"].at[side, gd, yd, :], (dx, dy, dz)))
-        for dx, dy in sorted(XY8, key=lambda d: -abs(d[0]) - abs(d[1])):
+                msgs2.append(post(b["PZ2"].at[gs, along(XS2, dy), :], b["RZ2"].at[side, gd, yd, :], (dx, dy, dz)))
+
+        corners = [d for d in XY if d[0] and d[1]]
+        for dx, dy in corners:
+            packed2(dx, dy)
+        for dx, dy in [d for d in XY8 if d not in corners] + corners:
             msgs2.append(
                 post(
                     G2.at[along(XS2, dx, H2), along(XS2, dy, RO2), :],
@@ -503,6 +528,8 @@
                     (dx, dy, 0),
                 )
             )
+        for dx, dy in [d for d in XY if d not in corners]:
+            packed2(dx, dy)
         for m in msgs2:
             m.wait()
 

time: 70.2 us -> 70.4 us (level)
  no operation moved by 1% of the time
where the time goes in v6:
time: 70.4 us; the launch traced here: 69.4 us
  Pallas kernels  67.4 us (96%)
  local copies, waits for them, and re-layouts  2.02 us (3%)
    pallas_call x1, Pallas kernels, shards(): pl.pallas_call(kernel, out_shape=pltpu.VMEM(right_side.shape, F32), in_sp...  67.4 us
    unnamed x1, local copies, waits for them, and re-layouts  2.02 us

profile of v6, /device:TPU:0, one launch (start us, length us, event | category | flops | bytes accessed | tf_op | source)
XLA Modules:
  0.0 69.4 jit_solution(11480778904927959742)
XLA Ops:
  0.0 67.4 %shard_map.28 = f32[64,64,256]{2,1,0:T(8,128)S(1)} custom-call(f32[64,64,256]{2,1,0:T(8,128)} %g_hbm.1, f32[64,64,256]{2,1,0:T(8,128)} %v_hbm.1), custom_call_target="tpu_custom_call" | custom-call | tf_op jit(solution)/shard_map/pallas_call | solution.py:696
  67.4 2.0 %copy.4 = f32[64,64,256]{2,1,0:T(8,128)} copy(f32[64,64,256]{2,1,0:T(8,128)S(1)} %shard_map.28) | data formatting | bytes 8388608

commit v7 on v6

--- a/solution.py
+++ b/solution.py
@@ -385,6 +385,7 @@
                 b["D"][grp, ct * 8 : ct * 8 + 8] = dn
         G1 = b["G1"]
         msgs1 = []
+        near1, side1 = [], []
 
         def along(spec, k, off=0):
             return slice(spec[k][0] + off, spec[k][0] + off + spec[k][1])
@@ -392,30 +393,33 @@
         def packed1(dx, dy):
             n = XS1[dy][1]
             ys, gs = along(XS1, dy), along(GS1, dx)
-            msgs1.append(post(b["U"].at[gs, ys, :], b["RU1", dx, dy].at[:, 0:n, :], (dx, dy, 1)))
-            msgs1.append(post(b["D"].at[gs, ys, :], b["RD", dx, dy].at[:, 0:n, :], (dx, dy, -1)))
+            to = side1 if dx else near1
+            to.append(post(b["U"].at[gs, ys, :], b["RU1", dx, dy].at[:, 0:n, :], (dx, dy, 1)))
+            to.append(post(b["D"].at[gs, ys, :], b["RD", dx, dy].at[:, 0:n, :], (dx, dy, -1)))
 
         corners = [d for d in XY if d[0] and d[1]]
         for dx, dy in corners:
             packed1(dx, dy)
         for dx, dy in [d for d in XY8 if d not in corners] + corners:
             n = XS1[dy][1]
-            msgs1.append(
+            msgs1.append((dx,
                 post(G1.at[along(XS1, dx, H1), 0, along(XS1, dy, RO1), :], b["RT", dx, dy].at[:, 0:n, :], (dx, dy, 0))
-            )
+            ))
         for dx, dy in [d for d in XY if d not in corners]:
             packed1(dx, dy)
         for dx, dy in XY8:
             n = XS1[dy][1]
-            msgs1.append(post(b["U"].at[along(GS1, dx), along(XS1, dy), :], b["RU0", dx, dy].at[:, 0:n, :], (dx, dy, 0)))
+            (side1 if dx else near1).append(
+                post(b["U"].at[along(GS1, dx), along(XS1, dy), :], b["RU0", dx, dy].at[:, 0:n, :], (dx, dy, 0))
+            )
         sum_msgs = total_stage(2, total_wait(1, sum_msgs))
-        for m in msgs1:
-            m.wait()
+        for dx, m in msgs1:
+            m.wait_send()
 
         def add1(q, v):
             G1f[pl.ds(q, 8)] = G1f[pl.ds(q, 8)] + v
 
-        for dx, dy in XY:
+        def add_from(dx, dy):
             sx, n = XS1[dx]
             sy = XS1[dy][0]
             tiles = PAD8[XS1[dy][1]] // 8
@@ -479,8 +483,33 @@
 
             return emit
 
-        ring1(G1f, lambda a, beside, g: ((2.0 - W) * first) * a + (C6 * first) * beside, put1(WAf), -3, 37, 10)
-        ring1(WAf, lambda a, beside, g: g - 0.25 * (6.0 * a - beside), put1(WBf), -1, 32, 11)
+        def two_relaxed(lo, hi, per):
+            ring1(G1f, lambda a, beside, g: ((2.0 - W) * first) * a + (C6 * first) * beside, put1(WAf), lo, hi, per)
+
+        def defect1(lo, hi, per):
+            ring1(WAf, lambda a, beside, g: g - 0.25 * (6.0 * a - beside), put1(WBf), lo, hi, per)
+
+        for m in near1:
+            m.wait()
+        for dx, m in msgs1:
+            if dx == 0:
+                m.wait_recv()
+        for dy in (0, -1, 1):
+            add_from(0, dy)
+        two_relaxed(2, 30, 7)
+        defect1(3, 29, 13)
+        for m in side1:
+            m.wait()
+        for dx, m in msgs1:
+            if dx:
+                m.wait_recv()
+        for dx, dy in XY:
+            if dx:
+                add_from(dx, dy)
+        two_relaxed(-3, 2, 5)
+        two_relaxed(30, 37, 7)
+        defect1(-1, 3, 4)
+        defect1(29, 32, 3)
 
         def restrict1(i, _):
             for t in range(2):

time: 70.4 us -> 69.7 us (0.990)
  Pallas kernels: 67.4 us -> 66.4 us
    pallas_call x1, Pallas kernels: 67.4 us -> 66.4 us  [shards(): pl.pallas_call(kernel, out_shape=pltpu.VMEM(right_side.shape, F32), in_sp...]
where the time goes in v7:
time: 69.7 us; the launch traced here: 68.4 us
  Pallas kernels  66.4 us (95%)
  local copies, waits for them, and re-layouts  2.02 us (3%)
    pallas_call x1, Pallas kernels, shards(): pl.pallas_call(kernel, out_shape=pltpu.VMEM(right_side.shape, F32), in_sp...  66.4 us
    unnamed x1, local copies, waits for them, and re-layouts  2.02 us

profile of v7, /device:TPU:0, one launch (start us, length us, event | category | flops | bytes accessed | tf_op | source)
XLA Modules:
  0.0 68.4 jit_solution(7582545947121698856)
XLA Ops:
  0.0 66.4 %shard_map.28 = f32[64,64,256]{2,1,0:T(8,128)S(1)} custom-call(f32[64,64,256]{2,1,0:T(8,128)} %g_hbm.1, f32[64,64,256]{2,1,0:T(8,128)} %v_hbm.1), custom_call_target="tpu_custom_call" | custom-call | tf_op jit(solution)/shard_map/pallas_call | solution.py:725
  66.4 2.0 %copy.4 = f32[64,64,256]{2,1,0:T(8,128)} copy(f32[64,64,256]{2,1,0:T(8,128)S(1)} %shard_map.28) | data formatting | bytes 8388608

commit v8 on v7

--- a/solution.py
+++ b/solution.py
@@ -544,23 +544,26 @@
             gd = along(GS2, dx, 1 - 2 * dx)
             yd = along(XS2, dy, 8 - N2 * dy)
             for side, dz in ((0, 1), (1, -1)):
-                msgs2.append(post(b["PZ2"].at[gs, along(XS2, dy), :], b["RZ2"].at[side, gd, yd, :], (dx, dy, dz)))
+                msgs2.append((dx, post(b["PZ2"].at[gs, along(XS2, dy), :], b["RZ2"].at[side, gd, yd, :], (dx, dy, dz))))
 
         corners = [d for d in XY if d[0] and d[1]]
         for dx, dy in corners:
             packed2(dx, dy)
         for dx, dy in [d for d in XY8 if d not in corners] + corners:
-            msgs2.append(
+            msgs2.append((dx,
                 post(
                     G2.at[along(XS2, dx, H2), along(XS2, dy, RO2), :],
                     G2.at[along(XS2, dx, H2 - N2 * dx), along(XS2, dy, RO2 - N2 * dy), :],
                     (dx, dy, 0),
                 )
-            )
+            ))
         for dx, dy in [d for d in XY if d not in corners]:
             packed2(dx, dy)
-        for m in msgs2:
-            m.wait()
+        for dx, m in msgs2:
+            m.wait_send()
+        for dx, m in msgs2:
+            if dx == 0:
+                m.wait_recv()
 
         first2 = W / (6.0 * 0.0625)
 
@@ -581,7 +584,7 @@
                     VAf[r] = first2 * v
             return 0
 
-        lax.fori_loop(0, 4, spread, 0)
+        lax.fori_loop(1, 3, spread, 0)
 
         def coarse(Sf, Tf, lo, n, per):
             def step(i, _):
@@ -600,7 +603,16 @@
             lax.fori_loop(0, n // per, step, 0)
 
         src, dst = VAf, VBf
-        for lo, n, per in ((2, 28, 7), (2, 28, 7), (4, 24, 8), (4, 24, 8), (6, 20, 10)):
+        coarse(src, dst, 9, 14, 14)
+        for dx, m in msgs2:
+            if dx:
+                m.wait_recv()
+        spread(0, 0)
+        spread(3, 0)
+        coarse(src, dst, 2, 7, 7)
+        coarse(src, dst, 23, 7, 7)
+        src, dst = dst, src
+        for lo, n, per in ((2, 28, 7), (4, 24, 8), (4, 24, 8), (6, 20, 10)):
             coarse(src, dst, lo, n, per)
             src, dst = dst, src
 

time: 69.7 us -> 69.1 us (level)
  Pallas kernels: 66.4 us -> 65.7 us
where the time goes in v8:
time: 69.1 us; the launch traced here: 67.7 us
  Pallas kernels  65.7 us (95%)
  local copies, waits for them, and re-layouts  2.02 us (3%)
    pallas_call x1, Pallas kernels, shards(): pl.pallas_call(kernel, out_shape=pltpu.VMEM(right_side.shape, F32), in_sp...  65.7 us
    unnamed x1, local copies, waits for them, and re-layouts  2.02 us

profile of v8, /device:TPU:0, one launch (start us, length us, event | category | flops | bytes accessed | tf_op | source)
XLA Modules:
  0.0 67.7 jit_solution(1576075688437268970)
XLA Ops:
  0.0 65.7 %shard_map.28 = f32[64,64,256]{2,1,0:T(8,128)S(1)} custom-call(f32[64,64,256]{2,1,0:T(8,128)} %g_hbm.1, f32[64,64,256]{2,1,0:T(8,128)} %v_hbm.1), custom_call_target="tpu_custom_call" | custom-call | tf_op jit(solution)/shard_map/pallas_call | solution.py:737
  65.7 2.0 %copy.4 = f32[64,64,256]{2,1,0:T(8,128)} copy(f32[64,64,256]{2,1,0:T(8,128)S(1)} %shard_map.28) | data formatting | bytes 8388608
